TPU v7x, 32 devices: a whole 2x2x4 slice. The times are simulated.
32 devices in a mesh: freq: 4 (over z), tm: 4 (over x, core), grp: 2 (over y).
Axes of the slice: x: 2, y: 2, z: 4, core: 2. Of those that a mesh axis runs over, the one named last changes fastest.
Arguments:
- voltages: bfloat16 [4, 2, 1024, 4096], P(None, None, ('freq', 'grp'), 'tm'), may hold values from -6 to 6
- prior_gains: float32 [4, 2, 1024], P('freq'), may hold values from -4.2 to 4.2
- station_flags: int32 [512], replicated, may hold values 0 or 1
- ingest_map: int32 [512], replicated, may hold values from 0 to 511, each once
- station_coords: float32 [2, 512], replicated, may hold values from -40 to 40
- pointing: int32 [2, 256], replicated, may hold values from 0 to 63
- corr_channels: int32 [4], replicated, may hold values from 0 to 3, each once
- beam_channels: int32 [4], replicated, may hold values from 0 to 3, each once
Outputs:
- visibilities: float32 [4, 2, 1024, 1024], P('freq', None, 'grp', 'tm')
- solved_gains: float32 [4, 2, 1024], P('freq')
- tied_beams: bfloat16 [4, 2, 2, 256, 4096], P('freq', None, None, 'grp', 'tm')
Inputs may be any that keep to these rules, and one draw needn't show every extreme that they name: `ingest_map`: each station appears in exactly one ingest slot. `corr_channels`: each channel is handled by exactly one correlator slot. `beam_channels`: each channel is handled by exactly one beamformer slot.
All inputs are finite; a program needn't handle non-finite values.
Results may differ from a plain program's by a relative error of at most 0.0049.
Values may be sent and summed in bfloat16 or wider, within the bound.
A program may use at most 64 MiB of HBM per device.

v0:
```python
import functools
import math

import jax
import jax.numpy as jnp
from jax import lax
from jax.experimental import pallas as pl
from jax.experimental.pallas import tpu as pltpu
from jax.sharding import PartitionSpec as P

ITERS = 4
LANES = 128
grid_cells = 64.0
MESH = pl.DeviceIdType.MESH


def partner(index, mask, count):
    result, bit = 0, 1
    while bit < count:
        digit = (index // bit) % 2
        result = result + bit * ((1 - digit) if mask & bit else digit)
        bit *= 2
    return result


def nt_dot(a, b):
    return lax.dot_general(a, b, (((1,), (1,)), ((), ())), preferred_element_type=jnp.float32)


class Plan:
    def __init__(self, nf, nt, ng, per_input, samples):
        self.nf, self.nt, self.ng = nf, nt, ng
        self.per_input, self.samples = per_input, samples
        self.inputs = nf * ng * per_input
        self.rows = self.inputs // ng
        self.cols = self.inputs // nt
        self.blocks = self.cols // per_input
        self.row_tiles = nt // ng
        quarter = per_input // 4
        self.late = quarter if quarter % 16 == 0 else 0
        self.early = per_input - self.late
        step = min(per_input, 32)
        self.chunks = tuple((part, first, step) for first in range(0, per_input, step) for part in (0, 1))
        half = self.cols // 2
        early_rows, late_rows = self.blocks * self.early, self.blocks * self.late
        units = [(0, early_rows, 0, half), (0, early_rows, half, half)]
        if late_rows:
            units.append((early_rows, late_rows, 0, self.cols))
        self.units = tuple(units)
        segments = [(b * self.early, self.early, b * per_input) for b in range(self.blocks)]
        if self.late:
            base = self.blocks * self.early
            segments += [(base + b * self.late, self.late, b * per_input + self.early) for b in range(self.blocks)]
        self.segments = tuple(segments)

    def held_row(self, first):
        if first < self.early:
            return self.early, first
        return self.late, self.blocks * self.early + first - self.early

    def unit_shape(self, unit):
        _, seg, _, lanes = self.units[unit]
        return self.row_tiles * seg, lanes


def kernel(plan, *refs):
    nf, nt, ng = plan.nf, plan.nt, plan.ng
    nu = len(plan.units)
    operands, refs = refs[:8], refs[8:]
    vis_hbm, gains_out, beams_hbm = refs[:3]
    refs = refs[3:]

    def take(count):
        nonlocal refs
        taken, refs = refs[:count], refs[count:]
        return taken

    src, corr, keep, cosine, sine, to_held, to_natural, left, right, beams_out, vis_out, gram = take(12)
    priors, updates, z, gains = take(4)
    stage_a, landed_a, stage_b, landed_b = (take(nu) for _ in range(4))
    first_src, mid, second_src, landed = (take(nu) for _ in range(4))
    zs, zr, ys, yr, own_sem, qs, qr, us, ur, gs, gr, as_, ar, bs, br, fs, fr, ss, sr, out_sem, in_sem = take(21)
    held = refs
    voltages, prior, flags, slots, coords, pointing, corr_channels, beam_channels = held
    loads = [pltpu.make_async_copy(operands[i], held[i], in_sem.at[i]) for i in range(8)]
    for load in loads:
        load.start()
    f = lax.axis_index("freq")
    t = lax.axis_index("tm")
    g = lax.axis_index("grp")
    per_input, samples = plan.per_input, plan.samples
    inputs, rows, cols = plan.inputs, plan.rows, plan.cols
    stations = inputs // 2
    chunks = plan.chunks
    offsets = [(dt, dg) for dg in range(ng) for dt in range(nt) if (dt, dg) != (0, 0)]
    masks = list(range(nf - 1, 0, -1))
    peers = {k: partner(f, k, nf) for k in range(nf)}
    tiles = {d: partner(t, d, nt) for d in range(nt)}

    def group(dt, dg):
        return {"freq": f, "tm": (t + dt) % nt, "grp": (g + dg) % ng}

    def along_freq(k):
        return {"freq": peers[k], "tm": t, "grp": g}

    def along_tm(d):
        return {"freq": f, "tm": tiles[d], "grp": g}

    barrier = pltpu.get_barrier_semaphore()
    for k in masks:
        pl.semaphore_signal(barrier, inc=1, device_id=along_freq(k), device_id_type=MESH)
    for dt, dg in offsets:
        pl.semaphore_signal(barrier, inc=1, device_id=group(dt, dg), device_id_type=MESH)
    for load in loads:
        load.wait()

    slot_rows = jnp.broadcast_to(slots[...].astype(jnp.float32), (LANES, stations)).T
    flagged = jnp.zeros((stations, LANES), jnp.float32)
    for first in range(0, stations, LANES):
        lane = lax.broadcasted_iota(jnp.int32, (stations, LANES), 1) + first
        flag = flags[0:1, first : first + LANES].astype(jnp.float32)
        flagged += jnp.where(slot_rows == lane.astype(jnp.float32), flag, 0.0)
    flagged = jnp.sum(flagged, axis=1, keepdims=True)
    keep[...] = jnp.broadcast_to(1.0 - flagged, (stations, LANES))
    first_slot = pl.multiple_of(((f * ng + g) * per_input) % stations, per_input)
    kept = keep[pl.ds(first_slot, per_input), 0:1].astype(jnp.bfloat16)

    for k in masks + [0]:
        for part in (0, 1):
            src[peers[k], part] = voltages[beam_channels[peers[k]], part] * kept

    pl.semaphore_wait(barrier, len(masks) + len(offsets))

    def held_start(owner, member, first, count):
        block = owner * ng + member
        stride, constant = plan.held_row(first)
        start = (block // plan.blocks) * cols + (block % plan.blocks) * stride + constant
        return pl.multiple_of(start, math.gcd(math.gcd(cols, stride), math.gcd(constant, count)))

    def place(owner, chunk):
        part, first, count = chunk
        return corr.at[part, pl.ds(held_start(owner, g, first, count), count), :]

    def z_copy(k, ci):
        part, first, count = chunks[ci]
        return pltpu.make_async_remote_copy(
            src_ref=src.at[peers[k], part, pl.ds(first, count), :],
            dst_ref=place(f, chunks[ci]),
            send_sem=zs.at[k - 1, ci],
            recv_sem=zr.at[k - 1, ci],
            device_id=along_freq(k),
            device_id_type=MESH,
        )

    def y_copy(k, ci, dg):
        part, first, count = chunks[ci]
        spot = place(peers[k], chunks[ci])
        return pltpu.make_async_remote_copy(
            src_ref=src.at[f, part, pl.ds(first, count), :] if k == 0 else spot,
            dst_ref=spot,
            send_sem=ys.at[dg - 1, k, ci],
            recv_sem=yr.at[dg - 1, k, ci],
            device_id=group(0, dg),
            device_id_type=MESH,
        )

    def forward(k, ci):
        for dg in range(1, ng):
            y_copy(k, ci, dg).start()

    own_parts = [(0, plan.early)] + ([(plan.early, plan.late)] if plan.late else [])
    own_copies = [
        pltpu.make_async_copy(
            src.at[f, :, pl.ds(first, count), :],
            corr.at[:, pl.ds(held_start(f, g, first, count), count), :],
            own_sem.at[i],
        )
        for i, (first, count) in enumerate(own_parts)
    ]

    def prior_copy(k):
        return pltpu.make_async_remote_copy(
            src_ref=prior.at[0],
            dst_ref=priors.at[f],
            send_sem=qs.at[k - 1],
            recv_sem=qr.at[k - 1],
            device_id=along_freq(k),
            device_id_type=MESH,
        )

    all_chunks = range(len(chunks))
    early_chunks = [ci for ci in all_chunks if chunks[ci][1] < plan.early]
    late_chunks = [ci for ci in all_chunks if chunks[ci][1] >= plan.early]
    for ci in all_chunks:
        for k in masks:
            z_copy(k, ci).start()
        if ci == 0:
            for k in masks:
                prior_copy(k).start()
    for ci in all_chunks:
        forward(0, ci)
    for copy in own_copies:
        copy.start()
    priors[f] = prior[0]

    n_beams = pointing.shape[1]
    beams = n_beams // ng
    my_beam = beam_channels[f]
    permuted = len(plan.segments) > 1 and bool(plan.late)

    def natural(held_index):
        result = held_index
        for start, size, target in plan.segments:
            inside = (held_index >= start) & (held_index < start + size)
            result = jnp.where(inside, held_index + (target - start), result)
        return result

    if permuted:
        along_rows = lax.broadcasted_iota(jnp.int32, (cols, cols), 0)
        along_lanes = lax.broadcasted_iota(jnp.int32, (cols, cols), 1)
        to_held[...] = jnp.where(natural(along_lanes) == along_rows, 1.0, 0.0)
        to_natural[...] = jnp.where(natural(along_rows) == along_lanes, 1.0, 0.0)

    def reorder(row_vector, matrix):
        if not permuted:
            return row_vector
        moved = [
            jnp.dot(
                row_vector[:, first : first + cols],
                matrix[...],
                precision=lax.Precision.HIGHEST,
                preferred_element_type=jnp.float32,
            )
            for first in range(0, row_vector.shape[1], cols)
        ]
        return jnp.concatenate(moved, axis=1)

    def point_phases():
        ratio = 0.875 + 0.25 * (my_beam.astype(jnp.float32) + 0.5) / nf
        mine = pl.ds(pl.multiple_of(g * beams, beams), beams)
        east_dir, north_dir = (
            jnp.broadcast_to((pointing[d : d + 1, mine].astype(jnp.float32) + 0.5) / grid_cells - 0.5, (LANES, beams)).T
            for d in (0, 1)
        )
        east, north = (jnp.broadcast_to(coords[d : d + 1, :], (LANES, stations)).T for d in (0, 1))
        station = lax.broadcasted_iota(jnp.int32, (stations, LANES), 0)
        slot_east, slot_north = [], []
        for first in range(0, stations, LANES):
            lanes = slice(first, first + LANES)
            match = station == slots[0:1, lanes]
            slot_east.append(jnp.sum(jnp.where(match, east, 0.0), axis=0, keepdims=True))
            slot_north.append(jnp.sum(jnp.where(match, north, 0.0), axis=0, keepdims=True))
        where = jnp.concatenate(
            [jnp.concatenate(slot_east, axis=1), jnp.concatenate(slot_north, axis=1)] * 4, axis=0
        )
        where = reorder(where, to_held)
        for first in range(0, stations, LANES):
            lanes = slice(first, first + LANES)
            phase = 2.0 * math.pi * ratio * (east_dir * where[0:1, lanes] + north_dir * where[1:2, lanes])
            cosine[:, lanes] = jnp.cos(phase)
            sine[:, lanes] = jnp.sin(phase)

    point_phases()

    scale = 1.0 / (samples * nt)
    odds = list(range(nt - 1, 0, -2))
    evens = [d - 1 for d in odds]

    def a_copy(u):
        return pltpu.make_async_remote_copy(
            src_ref=stage_a[u],
            dst_ref=landed_a[u],
            send_sem=as_.at[u],
            recv_sem=ar.at[u],
            device_id=along_tm(1),
            device_id_type=MESH,
        )

    def b_copy(u, d):
        return pltpu.make_async_remote_copy(
            src_ref=stage_b[u].at[d // 2 - 1],
            dst_ref=landed_b[u].at[d // 2 - 1],
            send_sem=bs.at[u, d // 2 - 1],
            recv_sem=br.at[u, d // 2 - 1],
            device_id=along_tm(d),
            device_id_type=MESH,
        )

    def first_copy(u, k):
        return pltpu.make_async_remote_copy(
            src_ref=first_src[u].at[peers[k]],
            dst_ref=mid[u].at[f],
            send_sem=fs.at[u, k - 1],
            recv_sem=fr.at[u, k - 1],
            device_id=along_freq(k),
            device_id_type=MESH,
        )

    def second_copy(u, k):
        return pltpu.make_async_remote_copy(
            src_ref=second_src[u].at[k - 1],
            dst_ref=landed[u].at[f],
            send_sem=ss.at[u, k - 1],
            recv_sem=sr.at[u, k - 1],
            device_id=along_freq(k),
            device_id_type=MESH,
        )

    def gram_lanes(u, d):
        _, _, lane, lanes = plan.units[u]
        return pl.ds(pl.multiple_of(tiles[d] * cols + lane, LANES), lanes)

    def correlate(u):
        seg, seg_rows, lane, lanes = plan.units[u]

        def stacked(part):
            pieces = []
            for r in range(plan.row_tiles):
                start = pl.multiple_of(g * rows + r * cols + seg, math.gcd(cols, seg_rows))
                pieces.append(corr[part, pl.ds(start, seg_rows), :])
            return jnp.concatenate(pieces, axis=0)

        mine_r, mine_i = stacked(0), stacked(1)
        for odd, members in ((True, odds), (False, evens)):
            others = [
                jnp.concatenate([corr[part, gram_lanes(u, d), :] for d in members], axis=0) for part in (0, 1)
            ]
            real = (nt_dot(mine_r, others[0]) + nt_dot(mine_i, others[1])) * scale
            imag = (nt_dot(mine_i, others[0]) - nt_dot(mine_r, others[1])) * scale
            for part, value in ((0, real), (1, imag)):
                for j, d in enumerate(members):
                    for r in range(plan.row_tiles):
                        gram[part, r * cols + seg : r * cols + seg + seg_rows, gram_lanes(u, d)] = value[
                            r * seg_rows : (r + 1) * seg_rows, j * lanes : (j + 1) * lanes
                        ]
                if odd:
                    stage_a[u][part] = value.astype(jnp.bfloat16)
        a_copy(u).start()

    def from_gram(u, part, d):
        seg, seg_rows, _, _ = plan.units[u]
        return jnp.concatenate(
            [gram[part, r * cols + seg : r * cols + seg + seg_rows, gram_lanes(u, d)] for r in range(plan.row_tiles)],
            axis=0,
        )

    def sum_pair(u):
        lanes = plan.units[u][3]
        a_copy(u).wait_recv()
        for j, d in enumerate(evens):
            if d:
                for part in (0, 1):
                    theirs = landed_a[u][part, :, j * lanes : (j + 1) * lanes].astype(jnp.float32)
                    stage_b[u][d // 2 - 1, part] = (from_gram(u, part, d) + theirs).astype(jnp.bfloat16)
        for d in evens:
            if d:
                b_copy(u, d).start()

    def sum_rest(u):
        total_rows, lanes = plan.unit_shape(u)
        piece = total_rows // nf
        for d in evens:
            if d:
                b_copy(u, d).wait_recv()
        j = len(evens) - 1
        for part in (0, 1):
            total = from_gram(u, part, 0) + landed_a[u][part, :, j * lanes : (j + 1) * lanes].astype(jnp.float32)
            for d in evens:
                if d:
                    total = total + landed_b[u][d // 2 - 1, part].astype(jnp.float32)
            total = total.astype(jnp.bfloat16)
            for p in range(nf):
                first_src[u][p, part] = total[p * piece : (p + 1) * piece]
        mid[u][f] = first_src[u][f]
        for k in masks:
            first_copy(u, k).start()

    def source_of(slot):
        wanted = corr_channels[slot]
        source = 0
        for s in range(nf):
            source = jnp.where(beam_channels[s] == wanted, s, source)
        return source

    def hand_on(u):
        for k in masks:
            first_copy(u, k).wait_recv()
        for k in masks:
            second_src[u][k - 1] = mid[u][source_of(peers[k])]
        landed[u][f] = mid[u][source_of(f)]
        for k in masks:
            second_copy(u, k).start()

    for ci in early_chunks:
        for k in masks:
            z_copy(k, ci).wait_recv()
            forward(k, ci)
    for copy in own_copies:
        copy.wait()
    for ci in early_chunks:
        for k in range(nf):
            for dg in range(1, ng):
                y_copy(k, ci, dg).wait_recv()
    jobs = [(ci, k) for ci in late_chunks for k in masks]

    def forward_late(count):
        for ci, k in jobs[:count]:
            z_copy(k, ci).wait_recv()
            forward(k, ci)
        del jobs[:count]

    if plan.late:
        correlate(0)
        forward_late(nf - 2)
        sum_pair(0)
        forward_late(nf - 2)
        sum_rest(0)
    forward_late(len(jobs))
    for ci in late_chunks:
        for k in range(nf):
            for dg in range(1, ng):
                y_copy(k, ci, dg).wait_recv()
    last_units = [u for u in range(nu) if u > 0 or not plan.late]
    for u in last_units:
        correlate(u)

    for k in masks:
        prior_copy(k).wait_recv()
    slot_of_mine = 0
    for k in range(nf):
        slot_of_mine = jnp.where(corr_channels[k] == my_beam, k, slot_of_mine)
    z[...] = reorder(priors[slot_of_mine], to_held)
    slot = g * nt + t
    strip = LANES

    def update_copy(iteration, o):
        dt, dg = offsets[o]
        return pltpu.make_async_remote_copy(
            src_ref=updates.at[iteration, slot],
            dst_ref=updates.at[iteration, slot],
            send_sem=us.at[iteration, o],
            recv_sem=ur.at[iteration, o],
            device_id=group(dt, dg),
            device_id_type=MESH,
        )

    beside = {i: [] for i in range(ITERS)}
    beside[0] += [functools.partial(sum_pair, u) for u in last_units]
    if plan.late:
        beside[1].append(functools.partial(hand_on, 0))
    beside[2].append(functools.partial(sum_rest, last_units[0]))
    beside[3] += [functools.partial(sum_rest, u) for u in last_units[1:]]
    for iteration in range(ITERS):
        power = jnp.sum(z[...] * z[...]) + 1e-06

        def product(r, carry):
            here = pl.ds(pl.multiple_of(r * strip, strip), strip)
            total_r = jnp.zeros((strip, LANES), jnp.float32)
            total_i = jnp.zeros((strip, LANES), jnp.float32)
            for c in range(inputs // LANES):
                lanes = slice(c * LANES, (c + 1) * LANES)
                part_r = gram[0, here, lanes]
                part_i = gram[1, here, lanes]
                gain_r = z[0:1, lanes]
                gain_i = z[1:2, lanes]
                total_r += part_r * gain_r - part_i * gain_i
                total_i += part_i * gain_r + part_r * gain_i
            updates[iteration, slot, 0:1, here] = jnp.sum(total_r.T, axis=0, keepdims=True)
            updates[iteration, slot, 1:2, here] = jnp.sum(total_i.T, axis=0, keepdims=True)
            return carry

        lax.fori_loop(0, rows // strip, product, 0)
        for o in range(len(offsets)):
            update_copy(iteration, o).start()
        for work in beside[iteration]:
            work()
        for o in range(len(offsets)):
            update_copy(iteration, o).wait_recv()
        for h in range(ng):
            total = updates[iteration, h * nt]
            for other in range(1, nt):
                total = total + updates[iteration, h * nt + other]
            lanes = slice(h * rows, (h + 1) * rows)
            z[:, lanes] = 0.5 * (z[:, lanes] + inputs * total / power)

    gains[f] = reorder(z[...], to_natural)

    def gain_copy(k):
        return pltpu.make_async_remote_copy(
            src_ref=gains.at[f],
            dst_ref=gains.at[f],
            send_sem=gs.at[k - 1],
            recv_sem=gr.at[k - 1],
            device_id=along_freq(k),
            device_id_type=MESH,
        )

    factor = 1.0 / math.sqrt(stations)
    for p in (0, 1):
        gain_r = z[0:1, p * stations : (p + 1) * stations]
        gain_i = z[1:2, p * stations : (p + 1) * stations]
        denom = jnp.maximum(gain_r * gain_r + gain_i * gain_i, 0.5)
        along_r = gain_r / denom
        along_i = gain_i / denom
        cos = cosine[...]
        sin = sine[...]
        w_r = ((cos * along_r - sin * along_i) * factor).astype(jnp.bfloat16)
        w_i = (-(cos * along_i + sin * along_r) * factor).astype(jnp.bfloat16)
        left[p, 0:beams] = w_r
        left[p, beams:] = w_i
        right[p, 0:beams] = -w_i
        right[p, beams:] = w_r
    for k in masks:
        gain_copy(k).start()
    hand_on(last_units[0])

    beam_copies = [
        pltpu.make_async_copy(beams_out.at[:, p], beams_hbm.at[:, p], out_sem.at[p]) for p in (0, 1)
    ]

    def beamform(p):
        rows_p = slice(p * stations, (p + 1) * stations)
        result = jnp.dot(left[p], corr[0, rows_p, :], preferred_element_type=jnp.float32)
        result = result + jnp.dot(right[p], corr[1, rows_p, :], preferred_element_type=jnp.float32)
        result = result.astype(jnp.bfloat16)
        beams_out[0, p, 0] = result[:beams]
        beams_out[0, p, 1] = result[beams:]

    beamform(0)
    for u in last_units[1:]:
        hand_on(u)
    beamform(1)
    for copy in beam_copies:
        copy.start()

    for k in masks:
        gain_copy(k).wait_recv()
    gains_out[0] = gains[source_of(f)]

    for u in range(nu):
        for k in masks:
            second_copy(u, k).wait_recv()
    vis_copies = [pltpu.make_async_copy(vis_out.at[:, part], vis_hbm.at[:, part], out_sem.at[2 + part]) for part in (0, 1)]
    for part in (0, 1):
        strips = [
            jnp.concatenate([landed[u][p, part] for p in range(nf)], axis=0) for u in range(nu)
        ]
        for r in range(plan.row_tiles):
            tile_rows = []
            seg_rows = plan.units[0][1]
            here = slice(r * seg_rows, (r + 1) * seg_rows)
            tile_rows.append(jnp.concatenate([strips[0][here], strips[1][here]], axis=1))
            if plan.late:
                seg_rows = plan.units[2][1]
                tile_rows.append(strips[2][r * seg_rows : (r + 1) * seg_rows])
            tile = jnp.concatenate(tile_rows, axis=0)
            if not permuted:
                vis_out[0, part, r * cols : (r + 1) * cols, :] = tile
                continue
            tile = jnp.dot(
                tile, to_natural[...].astype(jnp.bfloat16), preferred_element_type=jnp.float32
            ).astype(jnp.bfloat16)
            for start, size, target in plan.segments:
                vis_out[0, part, r * cols + target : r * cols + target + size, :] = tile[start : start + size]
    for copy in vis_copies:
        copy.start()

    for k in masks:
        prior_copy(k).wait_send()
        gain_copy(k).wait_send()
    for ci in all_chunks:
        for k in masks:
            z_copy(k, ci).wait_send()
        for k in range(nf):
            for dg in range(1, ng):
                y_copy(k, ci, dg).wait_send()
    for u in range(nu):
        a_copy(u).wait_send()
        for d in evens:
            if d:
                b_copy(u, d).wait_send()
        for k in masks:
            first_copy(u, k).wait_send()
            second_copy(u, k).wait_send()
    for iteration in range(ITERS):
        for o in range(len(offsets)):
            update_copy(iteration, o).wait_send()
    for copy in beam_copies + vis_copies:
        copy.wait()


def body(
    voltages,
    prior_gains,
    station_flags,
    ingest_map,
    station_coords,
    pointing,
    corr_channels,
    beam_channels,
):
    nf = lax.axis_size("freq")
    nt = lax.axis_size("tm")
    ng = lax.axis_size("grp")
    _, _, per_input, samples = voltages.shape
    stations = ingest_map.shape[0]
    plan = Plan(nf, nt, ng, per_input, samples)
    inputs, rows, cols = plan.inputs, plan.rows, plan.cols
    part_beams = pointing.shape[1] // ng
    nc, nu = len(plan.chunks), len(plan.units)
    pairs = nt // 2
    dma = pltpu.SemaphoreType.DMA
    vmem = pl.BlockSpec(memory_space=pltpu.VMEM)
    hbm = pl.BlockSpec(memory_space=pltpu.HBM)
    shapes = [plan.unit_shape(u) for u in range(nu)]

    def bf16(*shape):
        return pltpu.VMEM(shape, jnp.bfloat16)

    def f32(*shape):
        return pltpu.VMEM(shape, jnp.float32)

    vis, gains, beams = pl.pallas_call(
        functools.partial(kernel, plan),
        out_shape=(
            jax.ShapeDtypeStruct((1, 2, rows, cols), jnp.bfloat16),
            jax.ShapeDtypeStruct((1, 2, inputs), jnp.float32),
            jax.ShapeDtypeStruct((1, 2, 2, part_beams, samples), jnp.bfloat16),
        ),
        in_specs=[hbm] * 8,
        out_specs=(hbm, vmem, hbm),
        scratch_shapes=[
            bf16(nf, 2, per_input, samples),
            bf16(2, inputs, samples),
            f32(stations, LANES),
            f32(part_beams, stations),
            f32(part_beams, stations),
            f32(cols, cols),
            f32(cols, cols),
            bf16(2, 2 * part_beams, stations),
            bf16(2, 2 * part_beams, stations),
            bf16(1, 2, 2, part_beams, samples),
            bf16(1, 2, rows, cols),
            f32(2, rows, inputs),
            f32(nf, 2, inputs),
            f32(ITERS, ng * nt, 2, rows),
            f32(2, inputs),
            f32(nf, 2, inputs),
        ]
        + [bf16(2, r, pairs * w) for r, w in shapes] * 2
        + [bf16(pairs - 1, 2, r, w) for r, w in shapes] * 2
        + [bf16(nf, 2, r // nf, w) for r, w in shapes] * 2
        + [bf16(nf - 1, 2, r // nf, w) for r, w in shapes]
        + [bf16(nf, 2, r // nf, w) for r, w in shapes]
        + [
            dma((nf - 1, nc)),
            dma((nf - 1, nc)),
            dma((ng - 1, nf, nc)),
            dma((ng - 1, nf, nc)),
            dma((2,)),
            dma((nf - 1,)),
            dma((nf - 1,)),
            dma((ITERS, ng * nt - 1)),
            dma((ITERS, ng * nt - 1)),
            dma((nf - 1,)),
            dma((nf - 1,)),
            dma((nu,)),
            dma((nu,)),
            dma((nu, pairs - 1)),
            dma((nu, pairs - 1)),
            dma((nu, nf - 1)),
            dma((nu, nf - 1)),
            dma((nu, nf - 1)),
            dma((nu, nf - 1)),
            dma((4,)),
            dma((8,)),
            pltpu.VMEM(voltages.shape, jnp.bfloat16),
            pltpu.VMEM(prior_gains.shape, jnp.float32),
            pltpu.VMEM((1, stations), jnp.int32),
            pltpu.VMEM((1, stations), jnp.int32),
            pltpu.VMEM(station_coords.shape, jnp.float32),
            pltpu.VMEM(pointing.shape, jnp.int32),
            pltpu.SMEM(corr_channels.shape, jnp.int32),
            pltpu.SMEM(beam_channels.shape, jnp.int32),
        ],
        compiler_params=pltpu.CompilerParams(
            collective_id=0, has_side_effects=True, vmem_limit_bytes=67043328
        ),
    )(
        voltages,
        prior_gains,
        station_flags[None],
        ingest_map[None],
        station_coords,
        pointing,
        corr_channels,
        beam_channels,
    )
    return vis.astype(jnp.float32), gains, beams


def solution(mesh):
    return jax.shard_map(
        body,
        mesh=mesh,
        in_specs=(
            P(None, None, ("freq", "grp"), "tm"),
            P("freq", None, None),
            P(),
            P(),
            P(),
            P(),
            P(),
            P(),
        ),
        out_specs=(
            P("freq", None, "grp", "tm"),
            P("freq", None, None),
            P("freq", None, None, "grp", "tm"),
        ),
        check_vma=False,
    )
```

profile of v0, /device:TPU:0, one launch (start us, length us, event | category | flops | bytes accessed | tf_op | source)
XLA Modules:
  0.0 110.8 jit_solution(3311632278368184785)
XLA Ops:
  0.6 105.7 %shard_map.103 = (bf16[1,2,512,256]{3,2,1,0:T(8,128)(2,1)}, f32[1,2,1024]{2,1,0:T(2,128)}, bf16[1,2,2,128,1024]{4,3,2,1,0:T(8,128)(2,1)}) custom-call(bf16[4,2,128,1024]{3,2,1,0:T(8,128)(2,1)} %refs_0_.1, f32[1,2,1024]{2,1,0:T(2,128)} %refs_1_.1, s32[1,512]{1,0:T(1,128)} %bitcast.2, s32[1,512]{1,0:T(1,128)} %bitcast.3, f32[2,512]{1,0:T(2,128)} %refs_4_.1, ...), custom_call_target="tpu_custom_call" | custom-call | tf_op jit(solution)/shard_map/pallas_call | solution.py:623
  106.3 0.0 copy-start
  106.3 2.2 %convert_element_type.3 = f32[1,2,512,256]{3,2,1,0:T(8,128)} convert(bf16[1,2,512,256]{3,2,1,0:T(8,128)(2,1)} %get-tuple-element.6) | non-fusion elementwise | flops 262144 | bytes 1572864 | tf_op jit(solution)/shard_map/convert_element_type | solution.py:699
  108.5 1.3 %copy.13 = f32[1,2,1024]{2,1,0:T(2,128)} copy(f32[1,2,1024]{2,1,0:T(2,128)} %get-tuple-element.13) | data formatting | bytes 16384
  109.8 0.0 copy-done
  109.8 1.0 copy.14
Async XLA Ops:
  106.3 3.5 %copy-start = (bf16[1,2,2,128,1024]{4,3,2,1,0:T(8,128)(2,1)S(1)}, bf16[1,2,2,128,1024]{4,3,2,1,0:T(8,128)(2,1)}, u32[]{:S(2)}) copy-start(bf16[1,2,2,128,1024]{4,3,2,1,0:T(8,128)(2,1)} %get-tuple-element.14) | copy-start | bytes 3145732
where the time goes:
time: 111 us
  Pallas kernels  106 us (95%)
  local copies, waits for them, and re-layouts  2.27 us (2%)
  other arithmetic  2.18 us (2%)
    pallas_call x1, Pallas kernels, body(): pl.pallas_call(functools.partial(kernel, plan), out_shape=(jax.ShapeDtype...  106 us
    unnamed x4, local copies, waits for them, and re-layouts  2.27 us

commit v1 on v0

--- a/solution.py
+++ b/solution.py
@@ -36,31 +36,28 @@
         self.cols = self.inputs // nt
         self.blocks = self.cols // per_input
         self.row_tiles = nt // ng
-        quarter = per_input // 4
-        self.late = quarter if quarter % 16 == 0 else 0
-        self.early = per_input - self.late
-        step = min(per_input, 32)
-        self.chunks = tuple((part, first, step) for first in range(0, per_input, step) for part in (0, 1))
-        half = self.cols // 2
-        early_rows, late_rows = self.blocks * self.early, self.blocks * self.late
-        units = [(0, early_rows, 0, half), (0, early_rows, half, half)]
-        if late_rows:
-            units.append((early_rows, late_rows, 0, self.cols))
+        self.levels = 4 if per_input % 64 == 0 else 1
+        self.step = per_input // self.levels
+        self.level_rows = self.cols // self.levels
+        self.chunks = tuple((part, q * self.step, self.step) for q in range(self.levels) for part in (0, 1))
+        half, tiles = self.cols // 2, tuple(range(self.row_tiles))
+        if self.levels > 1:
+            most = self.cols - self.level_rows
+            units = [(tiles, 0, most, 0, half)]
+            units += [((r,), 0, most, half, half) for r in tiles]
+            units += [(tiles, most, self.level_rows, 0, self.cols)]
+        else:
+            units = [(tiles, 0, self.cols, 0, half), (tiles, 0, self.cols, half, half)]
         self.units = tuple(units)
-        segments = [(b * self.early, self.early, b * per_input) for b in range(self.blocks)]
-        if self.late:
-            base = self.blocks * self.early
-            segments += [(base + b * self.late, self.late, b * per_input + self.early) for b in range(self.blocks)]
-        self.segments = tuple(segments)
-
-    def held_row(self, first):
-        if first < self.early:
-            return self.early, first
-        return self.late, self.blocks * self.early + first - self.early
+        self.segments = tuple(
+            (q * self.level_rows + b * self.step, self.step, b * per_input + q * self.step)
+            for q in range(self.levels)
+            for b in range(self.blocks)
+        )
 
     def unit_shape(self, unit):
-        _, seg, _, lanes = self.units[unit]
-        return self.row_tiles * seg, lanes
+        tiles, _, seg_rows, _, lanes = self.units[unit]
+        return len(tiles) * seg_rows, lanes
 
 
 def kernel(plan, *refs):
@@ -131,15 +128,15 @@
 
     pl.semaphore_wait(barrier, len(masks) + len(offsets))
 
-    def held_start(owner, member, first, count):
+    def held_start(owner, member, first):
         block = owner * ng + member
-        stride, constant = plan.held_row(first)
-        start = (block // plan.blocks) * cols + (block % plan.blocks) * stride + constant
-        return pl.multiple_of(start, math.gcd(math.gcd(cols, stride), math.gcd(constant, count)))
+        level = first // plan.step
+        start = (block // plan.blocks) * cols + level * plan.level_rows + (block % plan.blocks) * plan.step
+        return pl.multiple_of(start, plan.step)
 
     def place(owner, chunk):
         part, first, count = chunk
-        return corr.at[part, pl.ds(held_start(owner, g, first, count), count), :]
+        return corr.at[part, pl.ds(held_start(owner, g, first), count), :]
 
     def z_copy(k, ci):
         part, first, count = chunks[ci]
@@ -168,14 +165,13 @@
         for dg in range(1, ng):
             y_copy(k, ci, dg).start()
 
-    own_parts = [(0, plan.early)] + ([(plan.early, plan.late)] if plan.late else [])
     own_copies = [
         pltpu.make_async_copy(
-            src.at[f, :, pl.ds(first, count), :],
-            corr.at[:, pl.ds(held_start(f, g, first, count), count), :],
-            own_sem.at[i],
-        )
-        for i, (first, count) in enumerate(own_parts)
+            src.at[f, :, pl.ds(first, plan.step), :],
+            corr.at[:, pl.ds(held_start(f, g, first), plan.step), :],
+            own_sem.at[first // plan.step],
+        )
+        for first in range(0, per_input, plan.step)
     ]
 
     def prior_copy(k):
@@ -189,11 +185,15 @@
         )
 
     all_chunks = range(len(chunks))
-    early_chunks = [ci for ci in all_chunks if chunks[ci][1] < plan.early]
-    late_chunks = [ci for ci in all_chunks if chunks[ci][1] >= plan.early]
-    for ci in all_chunks:
-        for k in masks:
-            z_copy(k, ci).start()
+    ahead = 2
+
+    def send_chunk(ci):
+        if ci < len(chunks):
+            for k in masks:
+                z_copy(k, ci).start()
+
+    for ci in range(ahead):
+        send_chunk(ci)
         if ci == 0:
             for k in masks:
                 prior_copy(k).start()
@@ -206,7 +206,7 @@
     n_beams = pointing.shape[1]
     beams = n_beams // ng
     my_beam = beam_channels[f]
-    permuted = len(plan.segments) > 1 and bool(plan.late)
+    permuted = plan.levels > 1
 
     def natural(held_index):
         result = held_index
@@ -306,46 +306,60 @@
             device_id_type=MESH,
         )
 
-    def gram_lanes(u, d):
-        _, _, lane, lanes = plan.units[u]
-        return pl.ds(pl.multiple_of(tiles[d] * cols + lane, LANES), lanes)
-
-    def correlate(u):
-        seg, seg_rows, lane, lanes = plan.units[u]
-
+    def correlate(seg, seg_rows, lane, lanes):
         def stacked(part):
             pieces = []
             for r in range(plan.row_tiles):
-                start = pl.multiple_of(g * rows + r * cols + seg, math.gcd(cols, seg_rows))
+                start = pl.multiple_of(g * rows + r * cols + seg, plan.level_rows)
                 pieces.append(corr[part, pl.ds(start, seg_rows), :])
-            return jnp.concatenate(pieces, axis=0)
-
-        mine_r, mine_i = stacked(0), stacked(1)
-        for odd, members in ((True, odds), (False, evens)):
-            others = [
-                jnp.concatenate([corr[part, gram_lanes(u, d), :] for d in members], axis=0) for part in (0, 1)
-            ]
-            real = (nt_dot(mine_r, others[0]) + nt_dot(mine_i, others[1])) * scale
-            imag = (nt_dot(mine_i, others[0]) - nt_dot(mine_r, others[1])) * scale
-            for part, value in ((0, real), (1, imag)):
-                for j, d in enumerate(members):
-                    for r in range(plan.row_tiles):
-                        gram[part, r * cols + seg : r * cols + seg + seg_rows, gram_lanes(u, d)] = value[
-                            r * seg_rows : (r + 1) * seg_rows, j * lanes : (j + 1) * lanes
-                        ]
-                if odd:
-                    stage_a[u][part] = value.astype(jnp.bfloat16)
+            return pieces
+
+        mine = jnp.concatenate(stacked(0) + stacked(1), axis=0)
+        count = plan.row_tiles * seg_rows
+        others = [
+            jnp.concatenate(
+                [corr[part, tile * cols + lane : tile * cols + lane + lanes, :] for tile in range(nt)], axis=0
+            )
+            for part in (0, 1)
+        ]
+        with_r = nt_dot(mine, others[0])
+        with_i = nt_dot(mine, others[1])
+        real = (with_r[:count] + with_i[count:]) * scale
+        imag = (with_r[count:] - with_i[:count]) * scale
+        for part, value in ((0, real), (1, imag)):
+            for tile in range(nt):
+                for r in range(plan.row_tiles):
+                    gram[part, tile, r * cols + seg : r * cols + seg + seg_rows, lane : lane + lanes] = value[
+                        r * seg_rows : (r + 1) * seg_rows, tile * lanes : (tile + 1) * lanes
+                    ]
+
+    def correlate_level(q):
+        size = plan.level_rows
+        correlate(0, (q + 1) * size, q * size, size)
+        if q >= 2:
+            correlate(q * size, size, 0, 2 * size)
+        if q % 2:
+            correlate(q * size, size, (q - 1) * size, size)
+
+    def from_gram(u, part, d):
+        row_tiles, seg, seg_rows, lane, lanes = plan.units[u]
+        return jnp.concatenate(
+            [
+                gram[part, tiles[d], r * cols + seg : r * cols + seg + seg_rows, lane : lane + lanes]
+                for r in row_tiles
+            ],
+            axis=0,
+        )
+
+    def send_pair(u):
+        lanes = plan.units[u][4]
+        for j, d in enumerate(odds):
+            for part in (0, 1):
+                stage_a[u][part, :, j * lanes : (j + 1) * lanes] = from_gram(u, part, d).astype(jnp.bfloat16)
         a_copy(u).start()
 
-    def from_gram(u, part, d):
-        seg, seg_rows, _, _ = plan.units[u]
-        return jnp.concatenate(
-            [gram[part, r * cols + seg : r * cols + seg + seg_rows, gram_lanes(u, d)] for r in range(plan.row_tiles)],
-            axis=0,
-        )
-
     def sum_pair(u):
-        lanes = plan.units[u][3]
+        lanes = plan.units[u][4]
         a_copy(u).wait_recv()
         for j, d in enumerate(evens):
             if d:
@@ -391,38 +405,40 @@
         for k in masks:
             second_copy(u, k).start()
 
-    for ci in early_chunks:
+    def relay(ci):
         for k in masks:
             z_copy(k, ci).wait_recv()
             forward(k, ci)
-    for copy in own_copies:
-        copy.wait()
-    for ci in early_chunks:
-        for k in range(nf):
-            for dg in range(1, ng):
-                y_copy(k, ci, dg).wait_recv()
-    jobs = [(ci, k) for ci in late_chunks for k in masks]
-
-    def forward_late(count):
-        for ci, k in jobs[:count]:
-            z_copy(k, ci).wait_recv()
-            forward(k, ci)
-        del jobs[:count]
-
-    if plan.late:
-        correlate(0)
-        forward_late(nf - 2)
-        sum_pair(0)
-        forward_late(nf - 2)
-        sum_rest(0)
-    forward_late(len(jobs))
-    for ci in late_chunks:
-        for k in range(nf):
-            for dg in range(1, ng):
-                y_copy(k, ci, dg).wait_recv()
-    last_units = [u for u in range(nu) if u > 0 or not plan.late]
-    for u in last_units:
-        correlate(u)
+        send_chunk(ci + ahead)
+
+    def await_level(q):
+        own_copies[q].wait()
+        for ci in (2 * q, 2 * q + 1):
+            for k in range(nf):
+                for dg in range(1, ng):
+                    y_copy(k, ci, dg).wait_recv()
+
+    last = plan.levels - 1
+    early_units = [0] if last else []
+    late_units = [u for u in range(nu) if u not in early_units]
+    for q in range(plan.levels):
+        relay(2 * q)
+        if q:
+            await_level(q - 1)
+            correlate_level(q - 1)
+            if q == last:
+                for u in early_units:
+                    send_pair(u)
+        relay(2 * q + 1)
+        if q == last:
+            for u in early_units:
+                sum_pair(u)
+    await_level(last)
+    correlate_level(last)
+    for u in late_units:
+        send_pair(u)
+    for u in early_units:
+        sum_rest(u)
 
     for k in masks:
         prior_copy(k).wait_recv()
@@ -432,6 +448,7 @@
     z[...] = reorder(priors[slot_of_mine], to_held)
     slot = g * nt + t
     strip = LANES
+    per_tile = cols // LANES
 
     def update_copy(iteration, o):
         dt, dg = offsets[o]
@@ -444,12 +461,17 @@
             device_id_type=MESH,
         )
 
-    beside = {i: [] for i in range(ITERS)}
-    beside[0] += [functools.partial(sum_pair, u) for u in last_units]
-    if plan.late:
-        beside[1].append(functools.partial(hand_on, 0))
-    beside[2].append(functools.partial(sum_rest, last_units[0]))
-    beside[3] += [functools.partial(sum_rest, u) for u in last_units[1:]]
+    beside = {i: [] for i in range(ITERS + 1)}
+
+    def plan_work(iteration, work, u):
+        beside[min(iteration, ITERS)].append(functools.partial(work, u))
+
+    for u in early_units:
+        plan_work(1, hand_on, u)
+    for i, u in enumerate(late_units):
+        plan_work(i // 2, sum_pair, u)
+        plan_work(i // 2 + 1, sum_rest, u)
+        plan_work(i // 2 + 2, hand_on, u)
     for iteration in range(ITERS):
         power = jnp.sum(z[...] * z[...]) + 1e-06
 
@@ -459,8 +481,9 @@
             total_i = jnp.zeros((strip, LANES), jnp.float32)
             for c in range(inputs // LANES):
                 lanes = slice(c * LANES, (c + 1) * LANES)
-                part_r = gram[0, here, lanes]
-                part_i = gram[1, here, lanes]
+                tile, inner = c // per_tile, slice(c % per_tile * LANES, (c % per_tile + 1) * LANES)
+                part_r = gram[0, tile, here, inner]
+                part_i = gram[1, tile, here, inner]
                 gain_r = z[0:1, lanes]
                 gain_i = z[1:2, lanes]
                 total_r += part_r * gain_r - part_i * gain_i
@@ -512,7 +535,6 @@
         right[p, beams:] = w_r
     for k in masks:
         gain_copy(k).start()
-    hand_on(last_units[0])
 
     beam_copies = [
         pltpu.make_async_copy(beams_out.at[:, p], beams_hbm.at[:, p], out_sem.at[p]) for p in (0, 1)
@@ -526,12 +548,11 @@
         beams_out[0, p, 0] = result[:beams]
         beams_out[0, p, 1] = result[beams:]
 
-    beamform(0)
-    for u in last_units[1:]:
-        hand_on(u)
-    beamform(1)
-    for copy in beam_copies:
-        copy.start()
+    for work in beside[ITERS]:
+        work()
+    for p in (0, 1):
+        beamform(p)
+        beam_copies[p].start()
 
     for k in masks:
         gain_copy(k).wait_recv()
@@ -546,13 +567,15 @@
             jnp.concatenate([landed[u][p, part] for p in range(nf)], axis=0) for u in range(nu)
         ]
         for r in range(plan.row_tiles):
-            tile_rows = []
-            seg_rows = plan.units[0][1]
-            here = slice(r * seg_rows, (r + 1) * seg_rows)
-            tile_rows.append(jnp.concatenate([strips[0][here], strips[1][here]], axis=1))
-            if plan.late:
-                seg_rows = plan.units[2][1]
-                tile_rows.append(strips[2][r * seg_rows : (r + 1) * seg_rows])
+            most = plan.units[0][2]
+            here = slice(r * most, (r + 1) * most)
+            if permuted:
+                tile_rows = [
+                    jnp.concatenate([strips[0][here], strips[1 + r]], axis=1),
+                    strips[-1][r * plan.level_rows : (r + 1) * plan.level_rows],
+                ]
+            else:
+                tile_rows = [jnp.concatenate([strips[0][here], strips[1][here]], axis=1)]
             tile = jnp.concatenate(tile_rows, axis=0)
             if not permuted:
                 vis_out[0, part, r * cols : (r + 1) * cols, :] = tile
@@ -641,7 +664,7 @@
             bf16(2, 2 * part_beams, stations),
             bf16(1, 2, 2, part_beams, samples),
             bf16(1, 2, rows, cols),
-            f32(2, rows, inputs),
+            f32(2, nt, rows, cols),
             f32(nf, 2, inputs),
             f32(ITERS, ng * nt, 2, rows),
             f32(2, inputs),
@@ -657,7 +680,7 @@
             dma((nf - 1, nc)),
             dma((ng - 1, nf, nc)),
             dma((ng - 1, nf, nc)),
-            dma((2,)),
+            dma((plan.levels,)),
             dma((nf - 1,)),
             dma((nf - 1,)),
             dma((ITERS, ng * nt - 1)),

time: 111 us -> 100 us (0.901)
  Pallas kernels: 106 us -> 94.8 us
    pallas_call x1, Pallas kernels: 106 us -> 94.8 us  [body(): pl.pallas_call(functools.partial(kernel, plan), out_shape=(jax.ShapeDtype...]
where the time goes in v1:
time: 100 us; the launch traced here: 99.9 us
  Pallas kernels  94.8 us (95%)
  local copies, waits for them, and re-layouts  2.27 us (2%)
  other arithmetic  2.18 us (2%)
    pallas_call x1, Pallas kernels, body(): pl.pallas_call(functools.partial(kernel, plan), out_shape=(jax.ShapeDtype...  94.8 us
    unnamed x4, local copies, waits for them, and re-layouts  2.27 us
    convert_element_type x1, other arithmetic, body(): return (vis.astype(jnp.float32), gains, beams)  2.18 us

profile of v1, /device:TPU:0, one launch (start us, length us, event | category | flops | bytes accessed | tf_op | source)
XLA Modules:
  0.0 99.9 jit_solution(4273054910694430148)
XLA Ops:
  0.6 94.8 %shard_map.103 = (bf16[1,2,512,256]{3,2,1,0:T(8,128)(2,1)}, f32[1,2,1024]{2,1,0:T(2,128)}, bf16[1,2,2,128,1024]{4,3,2,1,0:T(8,128)(2,1)}) custom-call(bf16[4,2,128,1024]{3,2,1,0:T(8,128)(2,1)} %refs_0_.1, f32[1,2,1024]{2,1,0:T(2,128)} %refs_1_.1, s32[1,512]{1,0:T(1,128)} %bitcast.2, s32[1,512]{1,0:T(1,128)} %bitcast.3, f32[2,512]{1,0:T(2,128)} %refs_4_.1, ...), custom_call_target="tpu_custom_call" | custom-call | tf_op jit(solution)/shard_map/pallas_call | solution.py:646
  95.5 0.0 copy-start
  95.5 2.2 %convert_element_type.3 = f32[1,2,512,256]{3,2,1,0:T(8,128)} convert(bf16[1,2,512,256]{3,2,1,0:T(8,128)(2,1)} %get-tuple-element.6) | non-fusion elementwise | flops 262144 | bytes 1572864 | tf_op jit(solution)/shard_map/convert_element_type | solution.py:722
  97.6 1.3 %copy.13 = f32[1,2,1024]{2,1,0:T(2,128)} copy(f32[1,2,1024]{2,1,0:T(2,128)} %get-tuple-element.13) | data formatting | bytes 16384
  98.9 0.0 copy-done
  98.9 1.0 copy.14
Async XLA Ops:
  95.5 3.5 %copy-start = (bf16[1,2,2,128,1024]{4,3,2,1,0:T(8,128)(2,1)S(1)}, bf16[1,2,2,128,1024]{4,3,2,1,0:T(8,128)(2,1)}, u32[]{:S(2)}) copy-start(bf16[1,2,2,128,1024]{4,3,2,1,0:T(8,128)(2,1)} %get-tuple-element.14) | copy-start | bytes 3145732

commit v2 on v1

--- a/solution.py
+++ b/solution.py
@@ -39,12 +39,12 @@
         self.levels = 4 if per_input % 64 == 0 else 1
         self.step = per_input // self.levels
         self.level_rows = self.cols // self.levels
-        self.chunks = tuple((part, q * self.step, self.step) for q in range(self.levels) for part in (0, 1))
+        count = 16 if self.step % 16 == 0 else self.step
+        self.chunks = tuple((part, first, count) for first in range(0, per_input, count) for part in (0, 1))
         half, tiles = self.cols // 2, tuple(range(self.row_tiles))
         if self.levels > 1:
             most = self.cols - self.level_rows
-            units = [(tiles, 0, most, 0, half)]
-            units += [((r,), 0, most, half, half) for r in tiles]
+            units = [((r,), 0, most, lane, half) for lane in (0, half) for r in tiles]
             units += [(tiles, most, self.level_rows, 0, self.cols)]
         else:
             units = [(tiles, 0, self.cols, 0, half), (tiles, 0, self.cols, half, half)]
@@ -64,7 +64,7 @@
     nf, nt, ng = plan.nf, plan.nt, plan.ng
     nu = len(plan.units)
     operands, refs = refs[:8], refs[8:]
-    vis_hbm, gains_out, beams_hbm = refs[:3]
+    vis_hbm, gains_hbm, beams_hbm = refs[:3]
     refs = refs[3:]
 
     def take(count):
@@ -72,7 +72,7 @@
         taken, refs = refs[:count], refs[count:]
         return taken
 
-    src, corr, keep, cosine, sine, to_held, to_natural, left, right, beams_out, vis_out, gram = take(12)
+    src, corr, keep, cosine, sine, to_held, to_natural, left, right, beams_out, vis_out, gains_out, gram = take(13)
     priors, updates, z, gains = take(4)
     stage_a, landed_a, stage_b, landed_b = (take(nu) for _ in range(4))
     first_src, mid, second_src, landed = (take(nu) for _ in range(4))
@@ -103,6 +103,9 @@
     def along_tm(d):
         return {"freq": f, "tm": tiles[d], "grp": g}
 
+    def await_all(ref, sem):
+        pltpu.make_async_copy(ref, ref, sem).wait()
+
     barrier = pltpu.get_barrier_semaphore()
     for k in masks:
         pl.semaphore_signal(barrier, inc=1, device_id=along_freq(k), device_id_type=MESH)
@@ -132,7 +135,7 @@
         block = owner * ng + member
         level = first // plan.step
         start = (block // plan.blocks) * cols + level * plan.level_rows + (block % plan.blocks) * plan.step
-        return pl.multiple_of(start, plan.step)
+        return pl.multiple_of(start + first % plan.step, math.gcd(plan.step, 16))
 
     def place(owner, chunk):
         part, first, count = chunk
@@ -143,7 +146,7 @@
         return pltpu.make_async_remote_copy(
             src_ref=src.at[peers[k], part, pl.ds(first, count), :],
             dst_ref=place(f, chunks[ci]),
-            send_sem=zs.at[k - 1, ci],
+            send_sem=zs,
             recv_sem=zr.at[k - 1, ci],
             device_id=along_freq(k),
             device_id_type=MESH,
@@ -155,8 +158,8 @@
         return pltpu.make_async_remote_copy(
             src_ref=src.at[f, part, pl.ds(first, count), :] if k == 0 else spot,
             dst_ref=spot,
-            send_sem=ys.at[dg - 1, k, ci],
-            recv_sem=yr.at[dg - 1, k, ci],
+            send_sem=ys.at[dg - 1],
+            recv_sem=yr.at[first // plan.step],
             device_id=group(0, dg),
             device_id_type=MESH,
         )
@@ -178,8 +181,8 @@
         return pltpu.make_async_remote_copy(
             src_ref=prior.at[0],
             dst_ref=priors.at[f],
-            send_sem=qs.at[k - 1],
-            recv_sem=qr.at[k - 1],
+            send_sem=qs,
+            recv_sem=qr,
             device_id=along_freq(k),
             device_id_type=MESH,
         )
@@ -290,8 +293,8 @@
         return pltpu.make_async_remote_copy(
             src_ref=first_src[u].at[peers[k]],
             dst_ref=mid[u].at[f],
-            send_sem=fs.at[u, k - 1],
-            recv_sem=fr.at[u, k - 1],
+            send_sem=fs.at[u],
+            recv_sem=fr.at[u],
             device_id=along_freq(k),
             device_id_type=MESH,
         )
@@ -300,8 +303,8 @@
         return pltpu.make_async_remote_copy(
             src_ref=second_src[u].at[k - 1],
             dst_ref=landed[u].at[f],
-            send_sem=ss.at[u, k - 1],
-            recv_sem=sr.at[u, k - 1],
+            send_sem=ss.at[u],
+            recv_sem=sr.at[u],
             device_id=along_freq(k),
             device_id_type=MESH,
         )
@@ -397,51 +400,54 @@
         return source
 
     def hand_on(u):
-        for k in masks:
-            first_copy(u, k).wait_recv()
+        await_all(mid[u].at[pl.ds(0, nf - 1)], fr.at[u])
         for k in masks:
             second_src[u][k - 1] = mid[u][source_of(peers[k])]
         landed[u][f] = mid[u][source_of(f)]
         for k in masks:
             second_copy(u, k).start()
 
+    nearest_first = [1] + masks[:-1] if nf > 1 else []
+
     def relay(ci):
-        for k in masks:
+        for k in nearest_first:
             z_copy(k, ci).wait_recv()
             forward(k, ci)
         send_chunk(ci + ahead)
 
+    def of_level(q):
+        return [ci for ci in all_chunks if chunks[ci][1] // plan.step == q]
+
     def await_level(q):
         own_copies[q].wait()
-        for ci in (2 * q, 2 * q + 1):
-            for k in range(nf):
-                for dg in range(1, ng):
-                    y_copy(k, ci, dg).wait_recv()
+        await_all(corr.at[:, pl.ds(0, (ng - 1) * nf * plan.step), :], yr.at[q])
 
     last = plan.levels - 1
-    early_units = [0] if last else []
+    early_units = list(range(plan.row_tiles)) if last else []
     late_units = [u for u in range(nu) if u not in early_units]
     for q in range(plan.levels):
-        relay(2 * q)
+        members = of_level(q)
+        relay(members[0])
         if q:
             await_level(q - 1)
             correlate_level(q - 1)
-            if q == last:
-                for u in early_units:
-                    send_pair(u)
-        relay(2 * q + 1)
+        if q == last:
+            for u in early_units:
+                send_pair(u)
+        relay(members[1])
         if q == last:
             for u in early_units:
                 sum_pair(u)
+        for ci in members[2:]:
+            relay(ci)
+    for u in early_units:
+        sum_rest(u)
     await_level(last)
     correlate_level(last)
     for u in late_units:
         send_pair(u)
-    for u in early_units:
-        sum_rest(u)
-
-    for k in masks:
-        prior_copy(k).wait_recv()
+
+    await_all(priors.at[pl.ds(0, nf - 1)], qr)
     slot_of_mine = 0
     for k in range(nf):
         slot_of_mine = jnp.where(corr_channels[k] == my_beam, k, slot_of_mine)
@@ -455,8 +461,8 @@
         return pltpu.make_async_remote_copy(
             src_ref=updates.at[iteration, slot],
             dst_ref=updates.at[iteration, slot],
-            send_sem=us.at[iteration, o],
-            recv_sem=ur.at[iteration, o],
+            send_sem=us,
+            recv_sem=ur.at[iteration],
             device_id=group(dt, dg),
             device_id_type=MESH,
         )
@@ -466,11 +472,13 @@
     def plan_work(iteration, work, u):
         beside[min(iteration, ITERS)].append(functools.partial(work, u))
 
-    for u in early_units:
-        plan_work(1, hand_on, u)
     for i, u in enumerate(late_units):
         plan_work(i // 2, sum_pair, u)
+    for i, u in enumerate(late_units):
         plan_work(i // 2 + 1, sum_rest, u)
+    for u in early_units:
+        plan_work(0, hand_on, u)
+    for i, u in enumerate(late_units):
         plan_work(i // 2 + 2, hand_on, u)
     for iteration in range(ITERS):
         power = jnp.sum(z[...] * z[...]) + 1e-06
@@ -497,8 +505,7 @@
             update_copy(iteration, o).start()
         for work in beside[iteration]:
             work()
-        for o in range(len(offsets)):
-            update_copy(iteration, o).wait_recv()
+        await_all(updates.at[iteration, pl.ds(0, len(offsets))], ur.at[iteration])
         for h in range(ng):
             total = updates[iteration, h * nt]
             for other in range(1, nt):
@@ -512,8 +519,8 @@
         return pltpu.make_async_remote_copy(
             src_ref=gains.at[f],
             dst_ref=gains.at[f],
-            send_sem=gs.at[k - 1],
-            recv_sem=gr.at[k - 1],
+            send_sem=gs,
+            recv_sem=gr,
             device_id=along_freq(k),
             device_id_type=MESH,
         )
@@ -554,24 +561,23 @@
         beamform(p)
         beam_copies[p].start()
 
-    for k in masks:
-        gain_copy(k).wait_recv()
+    await_all(gains.at[pl.ds(0, nf - 1)], gr)
     gains_out[0] = gains[source_of(f)]
+    gains_write = pltpu.make_async_copy(gains_out, gains_hbm, out_sem.at[4])
+    gains_write.start()
 
     for u in range(nu):
-        for k in masks:
-            second_copy(u, k).wait_recv()
+        await_all(landed[u].at[pl.ds(0, nf - 1)], sr.at[u])
     vis_copies = [pltpu.make_async_copy(vis_out.at[:, part], vis_hbm.at[:, part], out_sem.at[2 + part]) for part in (0, 1)]
     for part in (0, 1):
         strips = [
             jnp.concatenate([landed[u][p, part] for p in range(nf)], axis=0) for u in range(nu)
         ]
         for r in range(plan.row_tiles):
-            most = plan.units[0][2]
-            here = slice(r * most, (r + 1) * most)
+            here = slice(r * cols, (r + 1) * cols)
             if permuted:
                 tile_rows = [
-                    jnp.concatenate([strips[0][here], strips[1 + r]], axis=1),
+                    jnp.concatenate([strips[r], strips[plan.row_tiles + r]], axis=1),
                     strips[-1][r * plan.level_rows : (r + 1) * plan.level_rows],
                 ]
             else:
@@ -588,27 +594,20 @@
     for copy in vis_copies:
         copy.start()
 
-    for k in masks:
-        prior_copy(k).wait_send()
-        gain_copy(k).wait_send()
-    for ci in all_chunks:
-        for k in masks:
-            z_copy(k, ci).wait_send()
-        for k in range(nf):
-            for dg in range(1, ng):
-                y_copy(k, ci, dg).wait_send()
+    await_all(priors.at[pl.ds(0, nf - 1)], qs)
+    await_all(gains.at[pl.ds(0, nf - 1)], gs)
+    await_all(src.at[pl.ds(0, nf - 1)], zs)
+    for dg in range(1, ng):
+        await_all(src, ys.at[dg - 1])
     for u in range(nu):
         a_copy(u).wait_send()
         for d in evens:
             if d:
                 b_copy(u, d).wait_send()
-        for k in masks:
-            first_copy(u, k).wait_send()
-            second_copy(u, k).wait_send()
-    for iteration in range(ITERS):
-        for o in range(len(offsets)):
-            update_copy(iteration, o).wait_send()
-    for copy in beam_copies + vis_copies:
+        await_all(mid[u].at[pl.ds(0, nf - 1)], fs.at[u])
+        await_all(landed[u].at[pl.ds(0, nf - 1)], ss.at[u])
+    await_all(updates.at[:, pl.ds(0, len(offsets))], us)
+    for copy in beam_copies + vis_copies + [gains_write]:
         copy.wait()
 
 
@@ -633,7 +632,6 @@
     nc, nu = len(plan.chunks), len(plan.units)
     pairs = nt // 2
     dma = pltpu.SemaphoreType.DMA
-    vmem = pl.BlockSpec(memory_space=pltpu.VMEM)
     hbm = pl.BlockSpec(memory_space=pltpu.HBM)
     shapes = [plan.unit_shape(u) for u in range(nu)]
 
@@ -651,7 +649,7 @@
             jax.ShapeDtypeStruct((1, 2, 2, part_beams, samples), jnp.bfloat16),
         ),
         in_specs=[hbm] * 8,
-        out_specs=(hbm, vmem, hbm),
+        out_specs=(hbm, hbm, hbm),
         scratch_shapes=[
             bf16(nf, 2, per_input, samples),
             bf16(2, inputs, samples),
@@ -664,6 +662,7 @@
             bf16(2, 2 * part_beams, stations),
             bf16(1, 2, 2, part_beams, samples),
             bf16(1, 2, rows, cols),
+            f32(1, 2, inputs),
             f32(2, nt, rows, cols),
             f32(nf, 2, inputs),
             f32(ITERS, ng * nt, 2, rows),
@@ -676,26 +675,26 @@
         + [bf16(nf - 1, 2, r // nf, w) for r, w in shapes]
         + [bf16(nf, 2, r // nf, w) for r, w in shapes]
         + [
+            dma,
             dma((nf - 1, nc)),
-            dma((nf - 1, nc)),
-            dma((ng - 1, nf, nc)),
-            dma((ng - 1, nf, nc)),
+            dma((ng - 1,)),
             dma((plan.levels,)),
-            dma((nf - 1,)),
-            dma((nf - 1,)),
-            dma((ITERS, ng * nt - 1)),
-            dma((ITERS, ng * nt - 1)),
-            dma((nf - 1,)),
-            dma((nf - 1,)),
+            dma((plan.levels,)),
+            dma,
+            dma,
+            dma,
+            dma((ITERS,)),
+            dma,
+            dma,
             dma((nu,)),
             dma((nu,)),
             dma((nu, pairs - 1)),
             dma((nu, pairs - 1)),
-            dma((nu, nf - 1)),
-            dma((nu, nf - 1)),
-            dma((nu, nf - 1)),
-            dma((nu, nf - 1)),
-            dma((4,)),
+            dma((nu,)),
+            dma((nu,)),
+            dma((nu,)),
+            dma((nu,)),
+            dma((5,)),
             dma((8,)),
             pltpu.VMEM(voltages.shape, jnp.bfloat16),
             pltpu.VMEM(prior_gains.shape, jnp.float32),

time: 100 us -> 92.1 us (0.921)
  Pallas kernels: 94.8 us -> 86.8 us
    pallas_call x1, Pallas kernels: 94.8 us -> 86.8 us  [body(): pl.pallas_call(functools.partial(kernel, plan), out_shape=(jax.ShapeDtype...]
where the time goes in v2:
time: 92.1 us; the launch traced here: 91.9 us
  Pallas kernels  86.8 us (94%)
  local copies, waits for them, and re-layouts  2.27 us (2%)
  other arithmetic  2.18 us (2%)
    pallas_call x1, Pallas kernels, body(): pl.pallas_call(functools.partial(kernel, plan), out_shape=(jax.ShapeDtype...  86.8 us
    unnamed x4, local copies, waits for them, and re-layouts  2.27 us
    convert_element_type x1, other arithmetic, body(): return (vis.astype(jnp.float32), gains, beams)  2.18 us

profile of v2, /device:TPU:0, one launch (start us, length us, event | category | flops | bytes accessed | tf_op | source)
XLA Modules:
  0.0 91.9 jit_solution(3178003562971454618)
XLA Ops:
  0.6 86.8 %shard_map.103 = (bf16[1,2,512,256]{3,2,1,0:T(8,128)(2,1)}, f32[1,2,1024]{2,1,0:T(2,128)}, bf16[1,2,2,128,1024]{4,3,2,1,0:T(8,128)(2,1)}) custom-call(bf16[4,2,128,1024]{3,2,1,0:T(8,128)(2,1)} %refs_0_.1, f32[1,2,1024]{2,1,0:T(2,128)} %refs_1_.1, s32[1,512]{1,0:T(1,128)} %bitcast.2, s32[1,512]{1,0:T(1,128)} %bitcast.3, f32[2,512]{1,0:T(2,128)} %refs_4_.1, ...), custom_call_target="tpu_custom_call" | custom-call | tf_op jit(solution)/shard_map/pallas_call | solution.py:644
  87.5 0.0 copy-start
  87.5 2.2 %convert_element_type.3 = f32[1,2,512,256]{3,2,1,0:T(8,128)} convert(bf16[1,2,512,256]{3,2,1,0:T(8,128)(2,1)} %get-tuple-element.6) | non-fusion elementwise | flops 262144 | bytes 1572864 | tf_op jit(solution)/shard_map/convert_element_type | solution.py:721
  89.6 1.3 %copy.13 = f32[1,2,1024]{2,1,0:T(2,128)} copy(f32[1,2,1024]{2,1,0:T(2,128)} %get-tuple-element.13) | data formatting | bytes 16384
  90.9 0.0 copy-done
  90.9 1.0 %copy.14 = bf16[1,2,2,128,1024]{4,3,2,1,0:T(8,128)(2,1)} copy(bf16[1,2,2,128,1024]{4,3,2,1,0:T(8,128)(2,1)S(1)} %copy-done) | data formatting | bytes 2097152
Async XLA Ops:
  87.5 3.5 %copy-start = (bf16[1,2,2,128,1024]{4,3,2,1,0:T(8,128)(2,1)S(1)}, bf16[1,2,2,128,1024]{4,3,2,1,0:T(8,128)(2,1)}, u32[]{:S(2)}) copy-start(bf16[1,2,2,128,1024]{4,3,2,1,0:T(8,128)(2,1)} %get-tuple-element.14) | copy-start | bytes 3145732

commit v3 on v2

--- a/solution.py
+++ b/solution.py
@@ -44,7 +44,8 @@
         half, tiles = self.cols // 2, tuple(range(self.row_tiles))
         if self.levels > 1:
             most = self.cols - self.level_rows
-            units = [((r,), 0, most, lane, half) for lane in (0, half) for r in tiles]
+            units = [(tiles, 0, half, 0, half), (tiles, half, most - half, 0, half)]
+            units += [((r,), 0, most, half, half) for r in tiles]
             units += [(tiles, most, self.level_rows, 0, self.cols)]
         else:
             units = [(tiles, 0, self.cols, 0, half), (tiles, 0, self.cols, half, half)]
@@ -409,11 +410,18 @@
 
     nearest_first = [1] + masks[:-1] if nf > 1 else []
 
-    def relay(ci):
+    sent = [ahead]
+
+    def send_until(count):
+        while sent[0] < count:
+            send_chunk(sent[0])
+            sent[0] += 1
+
+    def relay(ci, spare=0):
         for k in nearest_first:
             z_copy(k, ci).wait_recv()
             forward(k, ci)
-        send_chunk(ci + ahead)
+        send_until(ci + 1 + ahead + spare)
 
     def of_level(q):
         return [ci for ci in all_chunks if chunks[ci][1] // plan.step == q]
@@ -423,29 +431,32 @@
         await_all(corr.at[:, pl.ds(0, (ng - 1) * nf * plan.step), :], yr.at[q])
 
     last = plan.levels - 1
-    early_units = list(range(plan.row_tiles)) if last else []
+    early_units = [0, 1] if last else []
     late_units = [u for u in range(nu) if u not in early_units]
+    ready = {last - 1: [0], last: [1]} if last else {}
     for q in range(plan.levels):
         members = of_level(q)
-        relay(members[0])
+        relay(members[0], spare=1)
         if q:
             await_level(q - 1)
             correlate_level(q - 1)
-        if q == last:
-            for u in early_units:
-                send_pair(u)
+        for u in ready.get(q, []):
+            send_pair(u)
         relay(members[1])
-        if q == last:
-            for u in early_units:
-                sum_pair(u)
+        for u in ready.get(q, []):
+            sum_pair(u)
+            if u:
+                sum_rest(u - 1)
         for ci in members[2:]:
             relay(ci)
-    for u in early_units:
+    for u in early_units[1:]:
         sum_rest(u)
     await_level(last)
     correlate_level(last)
     for u in late_units:
         send_pair(u)
+    for u in early_units[:1]:
+        hand_on(u)
 
     await_all(priors.at[pl.ds(0, nf - 1)], qr)
     slot_of_mine = 0
@@ -476,7 +487,7 @@
         plan_work(i // 2, sum_pair, u)
     for i, u in enumerate(late_units):
         plan_work(i // 2 + 1, sum_rest, u)
-    for u in early_units:
+    for u in early_units[1:]:
         plan_work(0, hand_on, u)
     for i, u in enumerate(late_units):
         plan_work(i // 2 + 2, hand_on, u)
@@ -574,13 +585,17 @@
             jnp.concatenate([landed[u][p, part] for p in range(nf)], axis=0) for u in range(nu)
         ]
         for r in range(plan.row_tiles):
-            here = slice(r * cols, (r + 1) * cols)
             if permuted:
+                first, second = plan.units[0][2], plan.units[1][2]
+                early = jnp.concatenate(
+                    [strips[0][r * first : (r + 1) * first], strips[1][r * second : (r + 1) * second]], axis=0
+                )
                 tile_rows = [
-                    jnp.concatenate([strips[r], strips[plan.row_tiles + r]], axis=1),
+                    jnp.concatenate([early, strips[2 + r]], axis=1),
                     strips[-1][r * plan.level_rows : (r + 1) * plan.level_rows],
                 ]
             else:
+                here = slice(r * cols, (r + 1) * cols)
                 tile_rows = [jnp.concatenate([strips[0][here], strips[1][here]], axis=1)]
             tile = jnp.concatenate(tile_rows, axis=0)
             if not permuted:
@@ -609,6 +624,24 @@
     await_all(updates.at[:, pl.ds(0, len(offsets))], us)
     for copy in beam_copies + vis_copies + [gains_write]:
         copy.wait()
+
+
+def finish(vis_in, gains_in, beams_in, vis_out, gains_out, beams_out, narrow, wide, gains, beams, sem, out_sem):
+    takes = [pltpu.make_async_copy(vis_in.at[:, part], narrow.at[:, part], sem.at[part]) for part in (0, 1)]
+    takes += [pltpu.make_async_copy(beams_in.at[:, p], beams.at[:, p], sem.at[2 + p]) for p in (0, 1)]
+    takes.append(pltpu.make_async_copy(gains_in, gains, sem.at[4]))
+    puts = [pltpu.make_async_copy(wide.at[:, part], vis_out.at[:, part], out_sem.at[part]) for part in (0, 1)]
+    puts += [pltpu.make_async_copy(beams.at[:, p], beams_out.at[:, p], out_sem.at[2 + p]) for p in (0, 1)]
+    puts.append(pltpu.make_async_copy(gains, gains_out, out_sem.at[4]))
+    for take in takes:
+        take.start()
+    for i in range(5):
+        takes[i].wait()
+        if i < 2:
+            wide[:, i] = narrow[:, i].astype(jnp.float32)
+        puts[i].start()
+    for put in puts:
+        put.wait()
 
 
 def body(
@@ -718,7 +751,21 @@
         corr_channels,
         beam_channels,
     )
-    return vis.astype(jnp.float32), gains, beams
+    results = (jax.ShapeDtypeStruct(vis.shape, jnp.float32), gains, beams)
+    return pl.pallas_call(
+        finish,
+        out_shape=tuple(jax.ShapeDtypeStruct(r.shape, r.dtype) for r in results),
+        in_specs=[hbm] * 3,
+        out_specs=(hbm,) * 3,
+        scratch_shapes=[
+            bf16(*vis.shape),
+            f32(*vis.shape),
+            f32(*gains.shape),
+            bf16(*beams.shape),
+            dma((5,)),
+            dma((5,)),
+        ],
+    )(vis, gains, beams)
 
 
 def solution(mesh):

time: 92.1 us -> 89.2 us (0.969)
  local copies, waits for them, and re-layouts: 2.27 us -> 0 us
  other arithmetic: 2.18 us -> 0 us
  Pallas kernels: 86.8 us -> 88.4 us
    pallas_call x0 -> x1, Pallas kernels: none -> 2.39 us  [body(): pl.pallas_call(finish, out_shape=tuple((jax.ShapeDtypeStruct(r.shape, r.d...]
    unnamed x4 -> x0, local copies, waits for them, and re-layouts: 2.27 us -> none
    convert_element_type x1 -> x0, other arithmetic: 2.18 us -> none  [body(): return (vis.astype(jnp.float32), gains, beams)]
where the time goes in v3:
time: 89.2 us; the launch traced here: 89 us
  Pallas kernels  88.4 us (99%)
    pallas_call x1, Pallas kernels, body(): pl.pallas_call(functools.partial(kernel, plan), out_shape=(jax.ShapeDtype...  86 us
    pallas_call x1, Pallas kernels, body(): pl.pallas_call(finish, out_shape=tuple((jax.ShapeDtypeStruct(r.shape, r.d...  2.39 us

profile of v3, /device:TPU:0, one launch (start us, length us, event | category | flops | bytes accessed | tf_op | source)
XLA Modules:
  0.0 89.0 jit_solution(3642014308468862567)
XLA Ops:
  0.6 86.0 %shard_map.103 = (bf16[1,2,512,256]{3,2,1,0:T(8,128)(2,1)}, f32[1,2,1024]{2,1,0:T(2,128)}, bf16[1,2,2,128,1024]{4,3,2,1,0:T(8,128)(2,1)}) custom-call(bf16[4,2,128,1024]{3,2,1,0:T(8,128)(2,1)} %refs_0_.1, f32[1,2,1024]{2,1,0:T(2,128)} %refs_1_.1, s32[1,512]{1,0:T(1,128)} %bitcast.2, s32[1,512]{1,0:T(1,128)} %bitcast.3, f32[2,512]{1,0:T(2,128)} %refs_4_.1, ...), custom_call_target="tpu_custom_call" | custom-call | tf_op jit(solution)/shard_map/pallas_call | solution.py:677
  86.6 2.4 %shard_map.104 = (f32[1,2,512,256]{3,2,1,0:T(8,128)}, f32[1,2,1024]{2,1,0:T(2,128)}, bf16[1,2,2,128,1024]{4,3,2,1,0:T(8,128)(2,1)}) custom-call(bf16[1,2,512,256]{3,2,1,0:T(8,128)(2,1)} %get-tuple-element.6.vis_in, f32[1,2,1024]{2,1,0:T(2,128)} %get-tuple-element.7.gains_in, bf16[1,2,2,128,1024]{4,3,2,1,0:T(8,128)(2,1)} %get-tuple-element.8.beams_in), custom_call_target="tpu_custom_call" | custom-call | tf_op jit(solution)/shard_map/pallas_call | solution.py:755

commit v4 on v3

--- a/solution.py
+++ b/solution.py
@@ -41,14 +41,14 @@
         self.level_rows = self.cols // self.levels
         count = 16 if self.step % 16 == 0 else self.step
         self.chunks = tuple((part, first, count) for first in range(0, per_input, count) for part in (0, 1))
-        half, tiles = self.cols // 2, tuple(range(self.row_tiles))
+        half = self.cols // 2
         if self.levels > 1:
             most = self.cols - self.level_rows
-            units = [(tiles, 0, half, 0, half), (tiles, half, most - half, 0, half)]
-            units += [((r,), 0, most, half, half) for r in tiles]
-            units += [(tiles, most, self.level_rows, 0, self.cols)]
+            units = [(0, half, 0, half, False), (half, most - half, 0, half, False)]
+            units += [(0, most, lane, self.level_rows, True) for lane in (half, most)]
+            units += [(most, self.level_rows, 0, self.cols, False)]
         else:
-            units = [(tiles, 0, self.cols, 0, half), (tiles, 0, self.cols, half, half)]
+            units = [(0, self.cols, 0, half, False), (0, self.cols, half, half, False)]
         self.units = tuple(units)
         self.segments = tuple(
             (q * self.level_rows + b * self.step, self.step, b * per_input + q * self.step)
@@ -57,15 +57,15 @@
         )
 
     def unit_shape(self, unit):
-        tiles, _, seg_rows, _, lanes = self.units[unit]
-        return len(tiles) * seg_rows, lanes
+        _, seg_rows, _, lanes, beside = self.units[unit]
+        return (seg_rows, self.row_tiles * lanes) if beside else (self.row_tiles * seg_rows, lanes)
 
 
 def kernel(plan, *refs):
     nf, nt, ng = plan.nf, plan.nt, plan.ng
     nu = len(plan.units)
     operands, refs = refs[:8], refs[8:]
-    vis_hbm, gains_hbm, beams_hbm = refs[:3]
+    vis_out, gains_out, beams_out = refs[:3]
     refs = refs[3:]
 
     def take(count):
@@ -73,11 +73,11 @@
         taken, refs = refs[:count], refs[count:]
         return taken
 
-    src, corr, keep, cosine, sine, to_held, to_natural, left, right, beams_out, vis_out, gains_out, gram = take(13)
+    src, corr, keep, cosine, sine, to_held, to_natural, left, right, gram = take(10)
     priors, updates, z, gains = take(4)
     stage_a, landed_a, stage_b, landed_b = (take(nu) for _ in range(4))
     first_src, mid, second_src, landed = (take(nu) for _ in range(4))
-    zs, zr, ys, yr, own_sem, qs, qr, us, ur, gs, gr, as_, ar, bs, br, fs, fr, ss, sr, out_sem, in_sem = take(21)
+    zs, zr, ys, yr, own_sem, qs, qr, us, ur, gs, gr, as_, ar, bs, br, fs, fr, ss, sr, in_sem = take(20)
     held = refs
     voltages, prior, flags, slots, coords, pointing, corr_channels, beam_channels = held
     loads = [pltpu.make_async_copy(operands[i], held[i], in_sem.at[i]) for i in range(8)]
@@ -346,24 +346,24 @@
             correlate(q * size, size, (q - 1) * size, size)
 
     def from_gram(u, part, d):
-        row_tiles, seg, seg_rows, lane, lanes = plan.units[u]
+        seg, seg_rows, lane, lanes, side_by_side = plan.units[u]
         return jnp.concatenate(
             [
                 gram[part, tiles[d], r * cols + seg : r * cols + seg + seg_rows, lane : lane + lanes]
-                for r in row_tiles
+                for r in range(plan.row_tiles)
             ],
-            axis=0,
+            axis=1 if side_by_side else 0,
         )
 
     def send_pair(u):
-        lanes = plan.units[u][4]
+        lanes = plan.unit_shape(u)[1]
         for j, d in enumerate(odds):
             for part in (0, 1):
                 stage_a[u][part, :, j * lanes : (j + 1) * lanes] = from_gram(u, part, d).astype(jnp.bfloat16)
         a_copy(u).start()
 
     def sum_pair(u):
-        lanes = plan.units[u][4]
+        lanes = plan.unit_shape(u)[1]
         a_copy(u).wait_recv()
         for j, d in enumerate(evens):
             if d:
@@ -431,9 +431,9 @@
         await_all(corr.at[:, pl.ds(0, (ng - 1) * nf * plan.step), :], yr.at[q])
 
     last = plan.levels - 1
-    early_units = [0, 1] if last else []
-    late_units = [u for u in range(nu) if u not in early_units]
-    ready = {last - 1: [0], last: [1]} if last else {}
+    early_units = [0, 1, 2] if last else []
+    late_units = [u for u in range(nu) if u not in early_units][::-1]
+    ready = {last - 1: [0], last: [1, 2]} if last else {}
     for q in range(plan.levels):
         members = of_level(q)
         relay(members[0], spare=1)
@@ -445,24 +445,24 @@
         relay(members[1])
         for u in ready.get(q, []):
             sum_pair(u)
-            if u:
-                sum_rest(u - 1)
+        if q == last:
+            for u in early_units[:1]:
+                sum_rest(u)
         for ci in members[2:]:
             relay(ci)
     for u in early_units[1:]:
         sum_rest(u)
+    await_all(priors.at[pl.ds(0, nf - 1)], qr)
+    slot_of_mine = 0
+    for k in range(nf):
+        slot_of_mine = jnp.where(corr_channels[k] == my_beam, k, slot_of_mine)
+    z[...] = reorder(priors[slot_of_mine], to_held)
     await_level(last)
     correlate_level(last)
     for u in late_units:
         send_pair(u)
     for u in early_units[:1]:
         hand_on(u)
-
-    await_all(priors.at[pl.ds(0, nf - 1)], qr)
-    slot_of_mine = 0
-    for k in range(nf):
-        slot_of_mine = jnp.where(corr_channels[k] == my_beam, k, slot_of_mine)
-    z[...] = reorder(priors[slot_of_mine], to_held)
     slot = g * nt + t
     strip = LANES
     per_tile = cols // LANES
@@ -483,14 +483,14 @@
     def plan_work(iteration, work, u):
         beside[min(iteration, ITERS)].append(functools.partial(work, u))
 
-    for i, u in enumerate(late_units):
-        plan_work(i // 2, sum_pair, u)
-    for i, u in enumerate(late_units):
-        plan_work(i // 2 + 1, sum_rest, u)
+    for u in late_units:
+        plan_work(0, sum_pair, u)
     for u in early_units[1:]:
         plan_work(0, hand_on, u)
     for i, u in enumerate(late_units):
-        plan_work(i // 2 + 2, hand_on, u)
+        plan_work(i + 1, sum_rest, u)
+    for i, u in enumerate(late_units):
+        plan_work(i + 2, hand_on, u)
     for iteration in range(ITERS):
         power = jnp.sum(z[...] * z[...]) + 1e-06
 
@@ -536,6 +536,9 @@
             device_id_type=MESH,
         )
 
+    for k in masks:
+        gain_copy(k).start()
+
     factor = 1.0 / math.sqrt(stations)
     for p in (0, 1):
         gain_r = z[0:1, p * stations : (p + 1) * stations]
@@ -551,12 +554,6 @@
         left[p, beams:] = w_i
         right[p, 0:beams] = -w_i
         right[p, beams:] = w_r
-    for k in masks:
-        gain_copy(k).start()
-
-    beam_copies = [
-        pltpu.make_async_copy(beams_out.at[:, p], beams_hbm.at[:, p], out_sem.at[p]) for p in (0, 1)
-    ]
 
     def beamform(p):
         rows_p = slice(p * stations, (p + 1) * stations)
@@ -570,29 +567,26 @@
         work()
     for p in (0, 1):
         beamform(p)
-        beam_copies[p].start()
 
     await_all(gains.at[pl.ds(0, nf - 1)], gr)
     gains_out[0] = gains[source_of(f)]
-    gains_write = pltpu.make_async_copy(gains_out, gains_hbm, out_sem.at[4])
-    gains_write.start()
 
     for u in range(nu):
         await_all(landed[u].at[pl.ds(0, nf - 1)], sr.at[u])
-    vis_copies = [pltpu.make_async_copy(vis_out.at[:, part], vis_hbm.at[:, part], out_sem.at[2 + part]) for part in (0, 1)]
     for part in (0, 1):
         strips = [
             jnp.concatenate([landed[u][p, part] for p in range(nf)], axis=0) for u in range(nu)
         ]
         for r in range(plan.row_tiles):
             if permuted:
-                first, second = plan.units[0][2], plan.units[1][2]
+                first, second = plan.units[0][1], plan.units[1][1]
                 early = jnp.concatenate(
                     [strips[0][r * first : (r + 1) * first], strips[1][r * second : (r + 1) * second]], axis=0
                 )
+                side = slice(r * plan.level_rows, (r + 1) * plan.level_rows)
                 tile_rows = [
-                    jnp.concatenate([early, strips[2 + r]], axis=1),
-                    strips[-1][r * plan.level_rows : (r + 1) * plan.level_rows],
+                    jnp.concatenate([early, strips[2][:, side], strips[3][:, side]], axis=1),
+                    strips[4][side],
                 ]
             else:
                 here = slice(r * cols, (r + 1) * cols)
@@ -606,8 +600,6 @@
             ).astype(jnp.bfloat16)
             for start, size, target in plan.segments:
                 vis_out[0, part, r * cols + target : r * cols + target + size, :] = tile[start : start + size]
-    for copy in vis_copies:
-        copy.start()
 
     await_all(priors.at[pl.ds(0, nf - 1)], qs)
     await_all(gains.at[pl.ds(0, nf - 1)], gs)
@@ -622,24 +614,16 @@
         await_all(mid[u].at[pl.ds(0, nf - 1)], fs.at[u])
         await_all(landed[u].at[pl.ds(0, nf - 1)], ss.at[u])
     await_all(updates.at[:, pl.ds(0, len(offsets))], us)
-    for copy in beam_copies + vis_copies + [gains_write]:
-        copy.wait()
-
-
-def finish(vis_in, gains_in, beams_in, vis_out, gains_out, beams_out, narrow, wide, gains, beams, sem, out_sem):
-    takes = [pltpu.make_async_copy(vis_in.at[:, part], narrow.at[:, part], sem.at[part]) for part in (0, 1)]
-    takes += [pltpu.make_async_copy(beams_in.at[:, p], beams.at[:, p], sem.at[2 + p]) for p in (0, 1)]
-    takes.append(pltpu.make_async_copy(gains_in, gains, sem.at[4]))
-    puts = [pltpu.make_async_copy(wide.at[:, part], vis_out.at[:, part], out_sem.at[part]) for part in (0, 1)]
-    puts += [pltpu.make_async_copy(beams.at[:, p], beams_out.at[:, p], out_sem.at[2 + p]) for p in (0, 1)]
-    puts.append(pltpu.make_async_copy(gains, gains_out, out_sem.at[4]))
-    for take in takes:
-        take.start()
-    for i in range(5):
-        takes[i].wait()
-        if i < 2:
-            wide[:, i] = narrow[:, i].astype(jnp.float32)
-        puts[i].start()
+
+
+def finish(vis_in, gains_in, beams_in, vis_out, gains_out, beams_out, wide, sem):
+    puts = [pltpu.make_async_copy(beams_in, beams_out, sem.at[0]), pltpu.make_async_copy(gains_in, gains_out, sem.at[1])]
+    for put in puts:
+        put.start()
+    for part in (0, 1):
+        wide[:, part] = vis_in[:, part].astype(jnp.float32)
+        puts.append(pltpu.make_async_copy(wide.at[:, part], vis_out.at[:, part], sem.at[2 + part]))
+        puts[-1].start()
     for put in puts:
         put.wait()
 
@@ -666,6 +650,7 @@
     pairs = nt // 2
     dma = pltpu.SemaphoreType.DMA
     hbm = pl.BlockSpec(memory_space=pltpu.HBM)
+    vmem = pl.BlockSpec(memory_space=pltpu.VMEM)
     shapes = [plan.unit_shape(u) for u in range(nu)]
 
     def bf16(*shape):
@@ -673,16 +658,18 @@
 
     def f32(*shape):
         return pltpu.VMEM(shape, jnp.float32)
+
+    kept_bytes = 4 * rows * cols + 8 * inputs + 8 * part_beams * samples + 61440
 
     vis, gains, beams = pl.pallas_call(
         functools.partial(kernel, plan),
         out_shape=(
-            jax.ShapeDtypeStruct((1, 2, rows, cols), jnp.bfloat16),
-            jax.ShapeDtypeStruct((1, 2, inputs), jnp.float32),
-            jax.ShapeDtypeStruct((1, 2, 2, part_beams, samples), jnp.bfloat16),
+            pltpu.VMEM((1, 2, rows, cols), jnp.bfloat16),
+            pltpu.VMEM((1, 2, inputs), jnp.float32),
+            pltpu.VMEM((1, 2, 2, part_beams, samples), jnp.bfloat16),
         ),
         in_specs=[hbm] * 8,
-        out_specs=(hbm, hbm, hbm),
+        out_specs=(vmem, vmem, vmem),
         scratch_shapes=[
             bf16(nf, 2, per_input, samples),
             bf16(2, inputs, samples),
@@ -693,9 +680,6 @@
             f32(cols, cols),
             bf16(2, 2 * part_beams, stations),
             bf16(2, 2 * part_beams, stations),
-            bf16(1, 2, 2, part_beams, samples),
-            bf16(1, 2, rows, cols),
-            f32(1, 2, inputs),
             f32(2, nt, rows, cols),
             f32(nf, 2, inputs),
             f32(ITERS, ng * nt, 2, rows),
@@ -727,7 +711,6 @@
             dma((nu,)),
             dma((nu,)),
             dma((nu,)),
-            dma((5,)),
             dma((8,)),
             pltpu.VMEM(voltages.shape, jnp.bfloat16),
             pltpu.VMEM(prior_gains.shape, jnp.float32),
@@ -739,7 +722,7 @@
             pltpu.SMEM(beam_channels.shape, jnp.int32),
         ],
         compiler_params=pltpu.CompilerParams(
-            collective_id=0, has_side_effects=True, vmem_limit_bytes=67043328
+            collective_id=0, has_side_effects=True, vmem_limit_bytes=67043328 - kept_bytes
         ),
     )(
         voltages,
@@ -755,16 +738,13 @@
     return pl.pallas_call(
         finish,
         out_shape=tuple(jax.ShapeDtypeStruct(r.shape, r.dtype) for r in results),
-        in_specs=[hbm] * 3,
+        in_specs=[vmem] * 3,
         out_specs=(hbm,) * 3,
         scratch_shapes=[
-            bf16(*vis.shape),
             f32(*vis.shape),
-            f32(*gains.shape),
-            bf16(*beams.shape),
-            dma((5,)),
-            dma((5,)),
+            dma((4,)),
         ],
+        compiler_params=pltpu.CompilerParams(vmem_limit_bytes=4 * 1024 * 1024),
     )(vis, gains, beams)
 
 

time: 89.2 us -> 86 us (0.964)
  Pallas kernels: 88.4 us -> 85.2 us
    pallas_call x1, Pallas kernels: 86 us -> 83.9 us  [body(): pl.pallas_call(functools.partial(kernel, plan), out_shape=(pltpu.VMEM((1,...]
    pallas_call x1, Pallas kernels: 2.39 us -> 1.35 us  [body(): pl.pallas_call(finish, out_shape=tuple((jax.ShapeDtypeStruct(r.shape, r.d...]
where the time goes in v4:
time: 86 us; the launch traced here: 85.9 us
  Pallas kernels  85.2 us (99%)
    pallas_call x1, Pallas kernels, body(): pl.pallas_call(functools.partial(kernel, plan), out_shape=(pltpu.VMEM((1,...  83.9 us

profile of v4, /device:TPU:0, one launch (start us, length us, event | category | flops | bytes accessed | tf_op | source)
XLA Modules:
  0.0 85.9 jit_solution(12780707909094642156)
XLA Ops:
  0.6 83.9 %shard_map.103 = (bf16[1,2,512,256]{3,2,1,0:T(8,128)(2,1)S(1)}, f32[1,2,1024]{2,1,0:T(2,128)S(1)}, bf16[1,2,2,128,1024]{4,3,2,1,0:T(8,128)(2,1)S(1)}) custom-call(bf16[4,2,128,1024]{3,2,1,0:T(8,128)(2,1)} %refs_0_.1, f32[1,2,1024]{2,1,0:T(2,128)} %refs_1_.1, s32[1,512]{1,0:T(1,128)} %bitcast.2, s32[1,512]{1,0:T(1,128)} %bitcast.3, f32[2,512]{1,0:T(2,128)} %refs_4_.1, ...), custom_call_target="tpu_custom_call" | custom-call | tf_op jit(solution)/shard_map/pallas_call | solution.py:664
  84.5 1.4 %shard_map.104 = (f32[1,2,512,256]{3,2,1,0:T(8,128)}, f32[1,2,1024]{2,1,0:T(2,128)}, bf16[1,2,2,128,1024]{4,3,2,1,0:T(8,128)(2,1)}) custom-call(bf16[1,2,512,256]{3,2,1,0:T(8,128)(2,1)S(1)} %get-tuple-element.6.vis_in, f32[1,2,1024]{2,1,0:T(2,128)S(1)} %get-tuple-element.7.gains_in, bf16[1,2,2,128,1024]{4,3,2,1,0:T(8,128)(2,1)S(1)} %get-tuple-element.8.beams_in), custom_call_target="tpu_custom_call" | custom-call | tf_op jit(solution)/shard_map/pallas_call | solution.py:738

commit v5 on v4

--- a/solution.py
+++ b/solution.py
@@ -25,6 +25,19 @@
 
 def nt_dot(a, b):
     return lax.dot_general(a, b, (((1,), (1,)), ((), ())), preferred_element_type=jnp.float32)
+
+
+def exact_parts(values):
+    high = values.astype(jnp.bfloat16)
+    rest = values - high.astype(jnp.float32)
+    middle = rest.astype(jnp.bfloat16)
+    low = (rest - middle.astype(jnp.float32)).astype(jnp.bfloat16)
+    return jnp.concatenate([high, middle, low], axis=0)
+
+
+def add_parts(values):
+    count = values.shape[0] // 3
+    return (values[2 * count :] + values[count : 2 * count]) + values[:count]
 
 
 class Plan:
@@ -74,7 +87,7 @@
         return taken
 
     src, corr, keep, cosine, sine, to_held, to_natural, left, right, gram = take(10)
-    priors, updates, z, gains = take(4)
+    priors, updates, z, gains, first_gains, gathered = take(6)
     stage_a, landed_a, stage_b, landed_b = (take(nu) for _ in range(4))
     first_src, mid, second_src, landed = (take(nu) for _ in range(4))
     zs, zr, ys, yr, own_sem, qs, qr, us, ur, gs, gr, as_, ar, bs, br, fs, fr, ss, sr, in_sem = take(20)
@@ -222,22 +235,18 @@
     if permuted:
         along_rows = lax.broadcasted_iota(jnp.int32, (cols, cols), 0)
         along_lanes = lax.broadcasted_iota(jnp.int32, (cols, cols), 1)
-        to_held[...] = jnp.where(natural(along_lanes) == along_rows, 1.0, 0.0)
-        to_natural[...] = jnp.where(natural(along_rows) == along_lanes, 1.0, 0.0)
-
-    def reorder(row_vector, matrix):
+        to_held[...] = jnp.where(natural(along_lanes) == along_rows, 1.0, 0.0).astype(jnp.bfloat16)
+        to_natural[...] = jnp.where(natural(along_rows) == along_lanes, 1.0, 0.0).astype(jnp.bfloat16)
+
+    def reorder(rows_in, matrix):
         if not permuted:
-            return row_vector
+            return rows_in
+        parts = exact_parts(rows_in)
         moved = [
-            jnp.dot(
-                row_vector[:, first : first + cols],
-                matrix[...],
-                precision=lax.Precision.HIGHEST,
-                preferred_element_type=jnp.float32,
-            )
-            for first in range(0, row_vector.shape[1], cols)
+            jnp.dot(parts[:, first : first + cols], matrix[...], preferred_element_type=jnp.float32)
+            for first in range(0, rows_in.shape[1], cols)
         ]
-        return jnp.concatenate(moved, axis=1)
+        return add_parts(jnp.concatenate(moved, axis=1))
 
     def point_phases():
         ratio = 0.875 + 0.25 * (my_beam.astype(jnp.float32) + 0.5) / nf
@@ -255,7 +264,7 @@
             slot_east.append(jnp.sum(jnp.where(match, east, 0.0), axis=0, keepdims=True))
             slot_north.append(jnp.sum(jnp.where(match, north, 0.0), axis=0, keepdims=True))
         where = jnp.concatenate(
-            [jnp.concatenate(slot_east, axis=1), jnp.concatenate(slot_north, axis=1)] * 4, axis=0
+            [jnp.concatenate(slot_east, axis=1), jnp.concatenate(slot_north, axis=1)], axis=0
         )
         where = reorder(where, to_held)
         for first in range(0, stations, LANES):
@@ -266,6 +275,17 @@
 
     point_phases()
 
+    await_all(priors.at[pl.ds(0, nf - 1)], qr)
+    slot_of_mine = 0
+    for k in range(nf):
+        slot_of_mine = jnp.where(corr_channels[k] == my_beam, k, slot_of_mine)
+    z[...] = reorder(priors[slot_of_mine], to_held)
+    start_parts = exact_parts(z[...])
+    size = plan.level_rows
+    for q in range(plan.levels):
+        pieces = [start_parts[:, tile * cols + q * size : tile * cols + (q + 1) * size] for tile in range(nt)]
+        first_gains[q] = jnp.concatenate(pieces, axis=1)
+
     scale = 1.0 / (samples * nt)
     odds = list(range(nt - 1, 0, -2))
     evens = [d - 1 for d in odds]
@@ -274,7 +294,7 @@
         return pltpu.make_async_remote_copy(
             src_ref=stage_a[u],
             dst_ref=landed_a[u],
-            send_sem=as_.at[u],
+            send_sem=as_,
             recv_sem=ar.at[u],
             device_id=along_tm(1),
             device_id_type=MESH,
@@ -284,7 +304,7 @@
         return pltpu.make_async_remote_copy(
             src_ref=stage_b[u].at[d // 2 - 1],
             dst_ref=landed_b[u].at[d // 2 - 1],
-            send_sem=bs.at[u, d // 2 - 1],
+            send_sem=bs,
             recv_sem=br.at[u, d // 2 - 1],
             device_id=along_tm(d),
             device_id_type=MESH,
@@ -294,7 +314,7 @@
         return pltpu.make_async_remote_copy(
             src_ref=first_src[u].at[peers[k]],
             dst_ref=mid[u].at[f],
-            send_sem=fs.at[u],
+            send_sem=fs,
             recv_sem=fr.at[u],
             device_id=along_freq(k),
             device_id_type=MESH,
@@ -304,7 +324,7 @@
         return pltpu.make_async_remote_copy(
             src_ref=second_src[u].at[k - 1],
             dst_ref=landed[u].at[f],
-            send_sem=ss.at[u],
+            send_sem=ss,
             recv_sem=sr.at[u],
             device_id=along_freq(k),
             device_id_type=MESH,
@@ -345,6 +365,47 @@
         if q % 2:
             correlate(q * size, size, (q - 1) * size, size)
 
+    def gather_level(q):
+        pieces = [
+            jnp.concatenate([corr[part, tile * cols + q * size : tile * cols + (q + 1) * size, :] for tile in range(nt)], axis=0)
+            for part in (0, 1)
+        ]
+        with_r, with_i = (
+            add_parts(jnp.dot(first_gains[q], piece, preferred_element_type=jnp.float32)) for piece in pieces
+        )
+        real = with_r[0:1] + with_i[1:2]
+        imag = with_r[1:2] - with_i[0:1]
+        if q:
+            real = real + gathered[0:1]
+            imag = imag + gathered[1:2]
+        gathered[0:1] = real
+        gathered[1:2] = imag
+
+    def first_product():
+        parts = exact_parts(gathered[...] * scale)
+        mine = pl.ds(pl.multiple_of(g * rows, rows), rows)
+        with_r = add_parts(nt_dot(parts, corr[0, mine, :]))
+        with_i = add_parts(nt_dot(parts, corr[1, mine, :]))
+        updates[0, slot, 0:1] = with_r[0:1] - with_i[1:2]
+        updates[0, slot, 1:2] = with_r[1:2] + with_i[0:1]
+
+    slot = g * nt + t
+
+    def update_copy(iteration, o):
+        dt, dg = offsets[o]
+        return pltpu.make_async_remote_copy(
+            src_ref=updates.at[iteration, slot],
+            dst_ref=updates.at[iteration, slot],
+            send_sem=us,
+            recv_sem=ur.at[iteration],
+            device_id=group(dt, dg),
+            device_id_type=MESH,
+        )
+
+    def send_updates(iteration):
+        for o in range(len(offsets)):
+            update_copy(iteration, o).start()
+
     def from_gram(u, part, d):
         seg, seg_rows, lane, lanes, side_by_side = plan.units[u]
         return jnp.concatenate(
@@ -432,13 +493,14 @@
 
     last = plan.levels - 1
     early_units = [0, 1, 2] if last else []
-    late_units = [u for u in range(nu) if u not in early_units][::-1]
+    late_units = [u for u in range(nu) if u not in early_units]
     ready = {last - 1: [0], last: [1, 2]} if last else {}
     for q in range(plan.levels):
         members = of_level(q)
         relay(members[0], spare=1)
         if q:
             await_level(q - 1)
+            gather_level(q - 1)
             correlate_level(q - 1)
         for u in ready.get(q, []):
             send_pair(u)
@@ -452,45 +514,31 @@
             relay(ci)
     for u in early_units[1:]:
         sum_rest(u)
-    await_all(priors.at[pl.ds(0, nf - 1)], qr)
-    slot_of_mine = 0
-    for k in range(nf):
-        slot_of_mine = jnp.where(corr_channels[k] == my_beam, k, slot_of_mine)
-    z[...] = reorder(priors[slot_of_mine], to_held)
     await_level(last)
+    gather_level(last)
+    first_product()
+    send_updates(0)
     correlate_level(last)
     for u in late_units:
         send_pair(u)
     for u in early_units[:1]:
         hand_on(u)
-    slot = g * nt + t
     strip = LANES
     per_tile = cols // LANES
 
-    def update_copy(iteration, o):
-        dt, dg = offsets[o]
-        return pltpu.make_async_remote_copy(
-            src_ref=updates.at[iteration, slot],
-            dst_ref=updates.at[iteration, slot],
-            send_sem=us,
-            recv_sem=ur.at[iteration],
-            device_id=group(dt, dg),
-            device_id_type=MESH,
-        )
-
     beside = {i: [] for i in range(ITERS + 1)}
 
     def plan_work(iteration, work, u):
         beside[min(iteration, ITERS)].append(functools.partial(work, u))
 
     for u in late_units:
-        plan_work(0, sum_pair, u)
+        plan_work(1, sum_pair, u)
     for u in early_units[1:]:
-        plan_work(0, hand_on, u)
+        plan_work(1, hand_on, u)
+    for u in late_units:
+        plan_work(2, sum_rest, u)
     for i, u in enumerate(late_units):
-        plan_work(i + 1, sum_rest, u)
-    for i, u in enumerate(late_units):
-        plan_work(i + 2, hand_on, u)
+        plan_work(i + 3, hand_on, u)
     for iteration in range(ITERS):
         power = jnp.sum(z[...] * z[...]) + 1e-06
 
@@ -511,9 +559,9 @@
             updates[iteration, slot, 1:2, here] = jnp.sum(total_i.T, axis=0, keepdims=True)
             return carry
 
-        lax.fori_loop(0, rows // strip, product, 0)
-        for o in range(len(offsets)):
-            update_copy(iteration, o).start()
+        if iteration:
+            lax.fori_loop(0, rows // strip, product, 0)
+            send_updates(iteration)
         for work in beside[iteration]:
             work()
         await_all(updates.at[iteration, pl.ds(0, len(offsets))], ur.at[iteration])
@@ -538,6 +586,9 @@
 
     for k in masks:
         gain_copy(k).start()
+
+    for work in beside[ITERS]:
+        work()
 
     factor = 1.0 / math.sqrt(stations)
     for p in (0, 1):
@@ -563,13 +614,8 @@
         beams_out[0, p, 0] = result[:beams]
         beams_out[0, p, 1] = result[beams:]
 
-    for work in beside[ITERS]:
-        work()
     for p in (0, 1):
         beamform(p)
-
-    await_all(gains.at[pl.ds(0, nf - 1)], gr)
-    gains_out[0] = gains[source_of(f)]
 
     for u in range(nu):
         await_all(landed[u].at[pl.ds(0, nf - 1)], sr.at[u])
@@ -596,23 +642,24 @@
                 vis_out[0, part, r * cols : (r + 1) * cols, :] = tile
                 continue
             tile = jnp.dot(
-                tile, to_natural[...].astype(jnp.bfloat16), preferred_element_type=jnp.float32
+                tile, to_natural[...], preferred_element_type=jnp.float32
             ).astype(jnp.bfloat16)
             for start, size, target in plan.segments:
                 vis_out[0, part, r * cols + target : r * cols + target + size, :] = tile[start : start + size]
+
+    await_all(gains.at[pl.ds(0, nf - 1)], gr)
+    gains_out[0] = gains[source_of(f)]
 
     await_all(priors.at[pl.ds(0, nf - 1)], qs)
     await_all(gains.at[pl.ds(0, nf - 1)], gs)
     await_all(src.at[pl.ds(0, nf - 1)], zs)
     for dg in range(1, ng):
         await_all(src, ys.at[dg - 1])
-    for u in range(nu):
-        a_copy(u).wait_send()
-        for d in evens:
-            if d:
-                b_copy(u, d).wait_send()
-        await_all(mid[u].at[pl.ds(0, nf - 1)], fs.at[u])
-        await_all(landed[u].at[pl.ds(0, nf - 1)], ss.at[u])
+    await_all(gram.at[0, pl.ds(0, len(odds))], as_)
+    if len(odds) > 1:
+        await_all(gram.at[0, pl.ds(0, len(odds) - 1)], bs)
+    for sem in (fs, ss):
+        await_all(gram.at[0, 0, pl.ds(0, rows // nf * (nf - 1))], sem)
     await_all(updates.at[:, pl.ds(0, len(offsets))], us)
 
 
@@ -676,8 +723,8 @@
             f32(stations, LANES),
             f32(part_beams, stations),
             f32(part_beams, stations),
-            f32(cols, cols),
-            f32(cols, cols),
+            bf16(cols, cols),
+            bf16(cols, cols),
             bf16(2, 2 * part_beams, stations),
             bf16(2, 2 * part_beams, stations),
             f32(2, nt, rows, cols),
@@ -685,6 +732,8 @@
             f32(ITERS, ng * nt, 2, rows),
             f32(2, inputs),
             f32(nf, 2, inputs),
+            bf16(plan.levels, 6, inputs // plan.levels),
+            f32(2, samples),
         ]
         + [bf16(2, r, pairs * w) for r, w in shapes] * 2
         + [bf16(pairs - 1, 2, r, w) for r, w in shapes] * 2
@@ -703,13 +752,13 @@
             dma((ITERS,)),
             dma,
             dma,
+            dma,
             dma((nu,)),
+            dma,
+            dma((nu, pairs - 1)),
+            dma,
             dma((nu,)),
-            dma((nu, pairs - 1)),
-            dma((nu, pairs - 1)),
-            dma((nu,)),
-            dma((nu,)),
-            dma((nu,)),
+            dma,
             dma((nu,)),
             dma((8,)),
             pltpu.VMEM(voltages.shape, jnp.bfloat16),

time: 86 us -> 83.4 us (0.970)
  Pallas kernels: 85.2 us -> 82.6 us
    pallas_call x1, Pallas kernels: 83.9 us -> 81.2 us  [body(): pl.pallas_call(functools.partial(kernel, plan), out_shape=(pltpu.VMEM((1,...]
where the time goes in v5:
time: 83.4 us; the launch traced here: 83.2 us
  Pallas kernels  82.6 us (99%)
    pallas_call x1, Pallas kernels, body(): pl.pallas_call(functools.partial(kernel, plan), out_shape=(pltpu.VMEM((1,...  81.2 us

profile of v5, /device:TPU:0, one launch (start us, length us, event | category | flops | bytes accessed | tf_op | source)
XLA Modules:
  0.0 83.2 jit_solution(17065151947072369777)
XLA Ops:
  0.6 81.2 %shard_map.103 = (bf16[1,2,512,256]{3,2,1,0:T(8,128)(2,1)S(1)}, f32[1,2,1024]{2,1,0:T(2,128)S(1)}, bf16[1,2,2,128,1024]{4,3,2,1,0:T(8,128)(2,1)S(1)}) custom-call(bf16[4,2,128,1024]{3,2,1,0:T(8,128)(2,1)} %refs_0_.1, f32[1,2,1024]{2,1,0:T(2,128)} %refs_1_.1, s32[1,512]{1,0:T(1,128)} %bitcast.2, s32[1,512]{1,0:T(1,128)} %bitcast.3, f32[2,512]{1,0:T(2,128)} %refs_4_.1, ...), custom_call_target="tpu_custom_call" | custom-call | tf_op jit(solution)/shard_map/pallas_call | solution.py:711
  81.9 1.4 %shard_map.104 = (f32[1,2,512,256]{3,2,1,0:T(8,128)}, f32[1,2,1024]{2,1,0:T(2,128)}, bf16[1,2,2,128,1024]{4,3,2,1,0:T(8,128)(2,1)}) custom-call(bf16[1,2,512,256]{3,2,1,0:T(8,128)(2,1)S(1)} %get-tuple-element.6.vis_in, f32[1,2,1024]{2,1,0:T(2,128)S(1)} %get-tuple-element.7.gains_in, bf16[1,2,2,128,1024]{4,3,2,1,0:T(8,128)(2,1)S(1)} %get-tuple-element.8.beams_in), custom_call_target="tpu_custom_call" | custom-call | tf_op jit(solution)/shard_map/pallas_call | solution.py:787

commit v6 on v5

--- a/solution.py
+++ b/solution.py
@@ -59,7 +59,8 @@
             most = self.cols - self.level_rows
             units = [(0, half, 0, half, False), (half, most - half, 0, half, False)]
             units += [(0, most, lane, self.level_rows, True) for lane in (half, most)]
-            units += [(most, self.level_rows, 0, self.cols, False)]
+            rest = self.level_rows // 2
+            units += [(first, rest, 0, self.cols, False) for first in (most, most + rest)]
         else:
             units = [(0, self.cols, 0, half, False), (0, self.cols, half, half, False)]
         self.units = tuple(units)
@@ -204,16 +205,18 @@
     all_chunks = range(len(chunks))
     ahead = 2
 
-    def send_chunk(ci):
-        if ci < len(chunks):
+    sent = [0]
+
+    def send_until(count):
+        while sent[0] < min(count, len(chunks)):
             for k in masks:
-                z_copy(k, ci).start()
-
-    for ci in range(ahead):
-        send_chunk(ci)
-        if ci == 0:
-            for k in masks:
-                prior_copy(k).start()
+                z_copy(k, sent[0]).start()
+            sent[0] += 1
+
+    send_until(1)
+    for k in masks:
+        prior_copy(k).start()
+    send_until(ahead)
     for ci in all_chunks:
         forward(0, ci)
     for copy in own_copies:
@@ -469,14 +472,7 @@
         for k in masks:
             second_copy(u, k).start()
 
-    nearest_first = [1] + masks[:-1] if nf > 1 else []
-
-    sent = [ahead]
-
-    def send_until(count):
-        while sent[0] < count:
-            send_chunk(sent[0])
-            sent[0] += 1
+    nearest_first = masks[-1:] + masks[:-1]
 
     def relay(ci, spare=0):
         for k in nearest_first:
@@ -518,11 +514,11 @@
     gather_level(last)
     first_product()
     send_updates(0)
+    for u in early_units[:1]:
+        hand_on(u)
     correlate_level(last)
     for u in late_units:
         send_pair(u)
-    for u in early_units[:1]:
-        hand_on(u)
     strip = LANES
     per_tile = cols // LANES
 
@@ -538,7 +534,7 @@
     for u in late_units:
         plan_work(2, sum_rest, u)
     for i, u in enumerate(late_units):
-        plan_work(i + 3, hand_on, u)
+        plan_work(4 if i > 1 else 3, hand_on, u)
     for iteration in range(ITERS):
         power = jnp.sum(z[...] * z[...]) + 1e-06
 
@@ -617,35 +613,47 @@
     for p in (0, 1):
         beamform(p)
 
-    for u in range(nu):
+    def unpack(first, count, blocks_of):
+        for part in (0, 1):
+            for r in range(plan.row_tiles):
+                block = blocks_of(part, r)
+                if not permuted:
+                    vis_out[0, part, r * cols + first : r * cols + first + count, :] = block
+                    continue
+                block = jnp.dot(block, to_natural[...], preferred_element_type=jnp.float32).astype(jnp.bfloat16)
+                at = first
+                while at < first + count:
+                    start, extent, target = next(s for s in plan.segments if s[0] <= at < s[0] + s[1])
+                    run = min(start + extent, first + count) - at
+                    goal = r * cols + target + at - start
+                    vis_out[0, part, goal : goal + run, :] = block[at - first : at - first + run]
+                    at += run
+
+    def arrived(u, part):
+        return jnp.concatenate([landed[u][p, part] for p in range(nf)], axis=0)
+
+    def early_block(part, r):
+        top, below = arrived(0, part), arrived(1, part)
+        first, second = plan.units[0][1], plan.units[1][1]
+        if not permuted:
+            return jnp.concatenate([top[r * first : (r + 1) * first], below[r * second : (r + 1) * second]], axis=1)
+        left_half = jnp.concatenate(
+            [top[r * first : (r + 1) * first], below[r * second : (r + 1) * second]], axis=0
+        )
+        side = slice(r * plan.level_rows, (r + 1) * plan.level_rows)
+        return jnp.concatenate([left_half, arrived(2, part)[:, side], arrived(3, part)[:, side]], axis=1)
+
+    def late_block(u, part, r):
+        count = plan.units[u][1]
+        return arrived(u, part)[r * count : (r + 1) * count]
+
+    early_end = cols - plan.level_rows if permuted else cols
+    for u in range(4 if permuted else nu):
         await_all(landed[u].at[pl.ds(0, nf - 1)], sr.at[u])
-    for part in (0, 1):
-        strips = [
-            jnp.concatenate([landed[u][p, part] for p in range(nf)], axis=0) for u in range(nu)
-        ]
-        for r in range(plan.row_tiles):
-            if permuted:
-                first, second = plan.units[0][1], plan.units[1][1]
-                early = jnp.concatenate(
-                    [strips[0][r * first : (r + 1) * first], strips[1][r * second : (r + 1) * second]], axis=0
-                )
-                side = slice(r * plan.level_rows, (r + 1) * plan.level_rows)
-                tile_rows = [
-                    jnp.concatenate([early, strips[2][:, side], strips[3][:, side]], axis=1),
-                    strips[4][side],
-                ]
-            else:
-                here = slice(r * cols, (r + 1) * cols)
-                tile_rows = [jnp.concatenate([strips[0][here], strips[1][here]], axis=1)]
-            tile = jnp.concatenate(tile_rows, axis=0)
-            if not permuted:
-                vis_out[0, part, r * cols : (r + 1) * cols, :] = tile
-                continue
-            tile = jnp.dot(
-                tile, to_natural[...], preferred_element_type=jnp.float32
-            ).astype(jnp.bfloat16)
-            for start, size, target in plan.segments:
-                vis_out[0, part, r * cols + target : r * cols + target + size, :] = tile[start : start + size]
+    unpack(0, early_end, early_block)
+    for u in range(4, nu):
+        await_all(landed[u].at[pl.ds(0, nf - 1)], sr.at[u])
+        unpack(plan.units[u][0], plan.units[u][1], functools.partial(late_block, u))
 
     await_all(gains.at[pl.ds(0, nf - 1)], gr)
     gains_out[0] = gains[source_of(f)]

time: 83.4 us -> 82.9 us (level)
  no operation moved by 1% of the time
where the time goes in v6:
time: 82.9 us; the launch traced here: 82.8 us
  Pallas kernels  82.1 us (99%)
    pallas_call x1, Pallas kernels, body(): pl.pallas_call(functools.partial(kernel, plan), out_shape=(pltpu.VMEM((1,...  80.8 us

profile of v6, /device:TPU:0, one launch (start us, length us, event | category | flops | bytes accessed | tf_op | source)
XLA Modules:
  0.0 82.8 jit_solution(3037561808447710769)
XLA Ops:
  0.6 80.8 %shard_map.103 = (bf16[1,2,512,256]{3,2,1,0:T(8,128)(2,1)S(1)}, f32[1,2,1024]{2,1,0:T(2,128)S(1)}, bf16[1,2,2,128,1024]{4,3,2,1,0:T(8,128)(2,1)S(1)}) custom-call(bf16[4,2,128,1024]{3,2,1,0:T(8,128)(2,1)} %refs_0_.1, f32[1,2,1024]{2,1,0:T(2,128)} %refs_1_.1, s32[1,512]{1,0:T(1,128)} %bitcast.2, s32[1,512]{1,0:T(1,128)} %bitcast.3, f32[2,512]{1,0:T(2,128)} %refs_4_.1, ...), custom_call_target="tpu_custom_call" | custom-call | tf_op jit(solution)/shard_map/pallas_call | solution.py:719
  81.4 1.4 %shard_map.104 = (f32[1,2,512,256]{3,2,1,0:T(8,128)}, f32[1,2,1024]{2,1,0:T(2,128)}, bf16[1,2,2,128,1024]{4,3,2,1,0:T(8,128)(2,1)}) custom-call(bf16[1,2,512,256]{3,2,1,0:T(8,128)(2,1)S(1)} %get-tuple-element.6.vis_in, f32[1,2,1024]{2,1,0:T(2,128)S(1)} %get-tuple-element.7.gains_in, bf16[1,2,2,128,1024]{4,3,2,1,0:T(8,128)(2,1)S(1)} %get-tuple-element.8.beams_in), custom_call_target="tpu_custom_call" | custom-call | tf_op jit(solution)/shard_map/pallas_call | solution.py:795

commit v7 on v6

--- a/solution.py
+++ b/solution.py
@@ -647,6 +647,15 @@
         count = plan.units[u][1]
         return arrived(u, part)[r * count : (r + 1) * count]
 
+    await_all(priors.at[pl.ds(0, nf - 1)], qs)
+    await_all(src.at[pl.ds(0, nf - 1)], zs)
+    for dg in range(1, ng):
+        await_all(src, ys.at[dg - 1])
+    await_all(gram.at[0, pl.ds(0, len(odds))], as_)
+    if len(odds) > 1:
+        await_all(gram.at[0, pl.ds(0, len(odds) - 1)], bs)
+    await_all(updates.at[:, pl.ds(0, len(offsets))], us)
+
     early_end = cols - plan.level_rows if permuted else cols
     for u in range(4 if permuted else nu):
         await_all(landed[u].at[pl.ds(0, nf - 1)], sr.at[u])
@@ -658,17 +667,9 @@
     await_all(gains.at[pl.ds(0, nf - 1)], gr)
     gains_out[0] = gains[source_of(f)]
 
-    await_all(priors.at[pl.ds(0, nf - 1)], qs)
     await_all(gains.at[pl.ds(0, nf - 1)], gs)
-    await_all(src.at[pl.ds(0, nf - 1)], zs)
-    for dg in range(1, ng):
-        await_all(src, ys.at[dg - 1])
-    await_all(gram.at[0, pl.ds(0, len(odds))], as_)
-    if len(odds) > 1:
-        await_all(gram.at[0, pl.ds(0, len(odds) - 1)], bs)
     for sem in (fs, ss):
         await_all(gram.at[0, 0, pl.ds(0, rows // nf * (nf - 1))], sem)
-    await_all(updates.at[:, pl.ds(0, len(offsets))], us)
 
 
 def finish(vis_in, gains_in, beams_in, vis_out, gains_out, beams_out, wide, sem):

time: 82.9 us -> 82.9 us (level)
  no operation moved by 1% of the time
where the time goes in v7:
time: 82.9 us; the launch traced here: 82.7 us
  Pallas kernels  82.1 us (99%)
    pallas_call x1, Pallas kernels, body(): pl.pallas_call(functools.partial(kernel, plan), out_shape=(pltpu.VMEM((1,...  80.8 us

profile of v7, /device:TPU:0, one launch (start us, length us, event | category | flops | bytes accessed | tf_op | source)
XLA Modules:
  0.0 82.7 jit_solution(10652064315466721709)
XLA Ops:
  0.6 80.8 %shard_map.103 = (bf16[1,2,512,256]{3,2,1,0:T(8,128)(2,1)S(1)}, f32[1,2,1024]{2,1,0:T(2,128)S(1)}, bf16[1,2,2,128,1024]{4,3,2,1,0:T(8,128)(2,1)S(1)}) custom-call(bf16[4,2,128,1024]{3,2,1,0:T(8,128)(2,1)} %refs_0_.1, f32[1,2,1024]{2,1,0:T(2,128)} %refs_1_.1, s32[1,512]{1,0:T(1,128)} %bitcast.2, s32[1,512]{1,0:T(1,128)} %bitcast.3, f32[2,512]{1,0:T(2,128)} %refs_4_.1, ...), custom_call_target="tpu_custom_call" | custom-call | tf_op jit(solution)/shard_map/pallas_call | solution.py:720
  81.4 1.4 %shard_map.104 = (f32[1,2,512,256]{3,2,1,0:T(8,128)}, f32[1,2,1024]{2,1,0:T(2,128)}, bf16[1,2,2,128,1024]{4,3,2,1,0:T(8,128)(2,1)}) custom-call(bf16[1,2,512,256]{3,2,1,0:T(8,128)(2,1)S(1)} %get-tuple-element.6.vis_in, f32[1,2,1024]{2,1,0:T(2,128)S(1)} %get-tuple-element.7.gains_in, bf16[1,2,2,128,1024]{4,3,2,1,0:T(8,128)(2,1)S(1)} %get-tuple-element.8.beams_in), custom_call_target="tpu_custom_call" | custom-call | tf_op jit(solution)/shard_map/pallas_call | solution.py:796
